TPU v7x, 32 devices: a whole 2x2x4 slice. The times are simulated.
32 devices in a mesh: span: 2 (over y), tm: 16 (over z, x, core).
Axes of the slice: x: 2, y: 2, z: 4, core: 2. Of those that a mesh axis runs over, the one named last changes fastest.
Arguments:
- traces: bfloat16 [1024, 32768], P(None, ('span', 'tm')), parts along dimension 1, may hold values from -6 to 6
- templates: bfloat16 [256, 16, 512], P('tm'), may hold values from -6 to 6
- blocks: int32 [16, 4], replicated, may hold values from 0 to 7, all different within a row
Outputs:
- detection: float32 [16, 32768], P(None, ('span', 'tm')), parts along dimension 1
There are 2 independent parts, one for each index of `span`. A program takes and returns all parts, laid end to end along the dimension named above; an argument that names none is the same for every part. Nothing has to cross between parts.
Inputs may be any that keep to these rules, and one draw needn't show every extreme that they name: Each row lists 4 different channel blocks.
All inputs are finite; a program needn't handle non-finite values.
Results may differ from a plain program's by a relative error of at most 0.0003.
Values may be sent and summed in bfloat16 or wider, within the bound.
No kernel may reach another device: no remote copies, remote signals or barrier semaphores. Data moves between devices by JAX's collectives and lax.ppermute only.
A program may use at most 128 MiB of HBM per device.

v0:
```python
import math

import jax
import jax.numpy as jnp
from jax import lax
from jax.experimental import pallas as pl
from jax.experimental.pallas import tpu as pltpu
from jax.sharding import PartitionSpec as P


template_groups = 4
epsilon = 1e-06
LANES = 128


def from_behind(block, axis, distance):
    devices = range(lax.axis_size(axis))
    route = [(i - distance, i) for i in devices if i - distance in devices]
    return lax.ppermute(block, axis, route)


def tap_total(product, lag_count):
    members, tap_count, span_width = product.shape
    flattened = product.reshape(members, tap_count * span_width)
    flattened = jnp.pad(flattened, ((0, 0), (0, tap_count)))
    return flattened.reshape(members, tap_count, span_width + 1)[:, :, :lag_count].sum(axis=1)


def per_device_general(traces, templates, blocks):
    channels, lag_count = traces.shape
    local_taps, members, row_count = templates.shape
    listed = blocks.shape[1]
    block_rows = row_count // listed
    nblocks = channels // block_rows
    tap_count = local_taps * lax.axis_size("tm")
    incoming = from_behind(traces[:, :tap_count], "tm", -1)
    source = jnp.concatenate([traces, incoming], axis=1)
    span_width = source.shape[1]
    squares = (
        jnp.square(source.astype(jnp.float32)).reshape(nblocks, block_rows, span_width).sum(axis=1)
    )
    running = jnp.concatenate(
        [jnp.zeros((nblocks, 1), jnp.float32), jnp.cumsum(squares, axis=1)], axis=1
    )
    window = running[:, tap_count : tap_count + lag_count] - running[:, :lag_count]
    selector = (blocks[:, :, None] == jnp.arange(nblocks, dtype=jnp.int32)[None, None, :]).astype(
        jnp.float32
    )
    counting = selector.sum(axis=1)
    scale_factor = math.sqrt(tap_count * row_count)
    group_size = members // template_groups
    gathered = lax.all_gather(templates, "tm", axis=0, tiled=True)
    pieces = []
    norm_pieces = []
    for group_index in range(template_groups):
        offset = group_index * group_size
        weights = gathered[:, offset : offset + group_size]
        chosen = source.reshape(nblocks, block_rows, span_width)[
            blocks[offset : offset + group_size]
        ]
        chosen = chosen.reshape(group_size, row_count, span_width)
        product = jnp.einsum("kqr,qrl->qkl", weights, chosen, preferred_element_type=jnp.float32)
        pieces.append(tap_total(product, lag_count))
        norm_pieces.append(jnp.sum(jnp.square(weights.astype(jnp.float32)), axis=(0, 2)))
    correlation = jnp.concatenate(pieces, axis=0)
    norm_sums = jnp.concatenate(norm_pieces, axis=0)
    energy = jnp.dot(counting, window, precision=lax.Precision.HIGHEST)
    denominator = energy * norm_sums[:, None] + epsilon
    return correlation * lax.rsqrt(denominator) * scale_factor


SMEM = pl.BlockSpec(memory_space=pltpu.SMEM)
VMEM = pl.BlockSpec(memory_space=pltpu.VMEM)
HBM = pl.BlockSpec(memory_space=pltpu.HBM)
PARAMS = pltpu.CompilerParams(vmem_limit_bytes=24 << 20)


def resident(value):
    return pltpu.with_memory_space_constraint(value, pltpu.VMEM)


def in_hbm(value):
    return pltpu.with_memory_space_constraint(value, pltpu.HBM)


def roll_left(value, distance):
    width = value.shape[-1]
    return pltpu.roll(value, (width - distance) % width, axis=1)


def prepare(listing, traces, own, members, nblocks, tap_count):
    channels, lags = traces.shape
    rows = channels // nblocks
    listed = listing.shape[0]
    width = tap_count + lags

    def kernel(listing_ref, x_hbm, own_hbm, before_ref, energy_ref, mask_ref, x_ref, own_ref, sums, sems):
        copies = [
            pltpu.make_async_copy(x_hbm.at[pl.ds(b * rows, rows)], x_ref.at[pl.ds(b * rows, rows)], sems.at[b])
            for b in range(nblocks)
        ]
        copies.append(pltpu.make_async_copy(own_hbm, own_ref, sems.at[nblocks]))
        for copy in copies:
            copy.start()
        member = lax.broadcasted_iota(jnp.int32, (members, rows), 0)
        for m in range(listed):
            block = jnp.zeros((members, rows), jnp.int32)
            for j in range(members):
                block = jnp.where(member == j, listing_ref[m, j], block)
            for n in range(nblocks):
                mask_ref[m, n] = jnp.where(block == n, 1.0, 0.0).astype(jnp.bfloat16)
        sums[:, :tap_count] = jnp.zeros((nblocks, tap_count), jnp.float32)
        for b in range(nblocks):
            copies[b].wait()
            block = x_ref[b * rows : (b + 1) * rows, :].astype(jnp.float32)
            sums[b : b + 1, tap_count:] = jnp.sum(jnp.square(block), axis=0, keepdims=True)
        total = sums[...]
        distance = 1
        while distance < tap_count:
            total = total + roll_left(total, distance)
            distance *= 2
        sums[...] = total
        for j in range(members):
            energy = sums[pl.ds(listing_ref[0, j], 1), :]
            for m in range(1, listed):
                energy = energy + sums[pl.ds(listing_ref[m, j], 1), :]
            before_ref[j : j + 1, :] = energy[:, :tap_count]
            energy_ref[j : j + 1, :] = energy[:, tap_count:]
        copies[nblocks].wait()

    return pl.pallas_call(
        kernel,
        out_shape=(
            pltpu.VMEM((members, tap_count), jnp.float32),
            pltpu.VMEM((members, lags), jnp.float32),
            pltpu.VMEM((listed, nblocks, members, rows), jnp.bfloat16),
            pltpu.VMEM(traces.shape, traces.dtype),
            pltpu.VMEM(own.shape, own.dtype),
        ),
        in_specs=[SMEM, HBM, HBM],
        out_specs=(VMEM,) * 5,
        scratch_shapes=[pltpu.VMEM((nblocks, width), jnp.float32), pltpu.SemaphoreType.DMA((nblocks + 1,))],
        compiler_params=PARAMS,
        name="prepare",
    )(in_hbm(listing), in_hbm(traces), in_hbm(own))


def spread(mask_ref, raw_refs, wide, blocks):
    listed, _, members, rows = mask_ref.shape
    start = 0
    for raw_ref in raw_refs:
        flat = raw_ref.shape[0]
        for n in blocks:
            total = jnp.zeros((flat, rows), jnp.bfloat16)
            for m in range(listed):
                mask = (mask_ref[m, n] > 0)[None]
                mask = jnp.broadcast_to(mask, (flat // members, members, rows)).reshape(flat, rows)
                total = jnp.where(mask, raw_ref[:, m * rows : (m + 1) * rows], total)
            wide[start : start + flat, n * rows : (n + 1) * rows] = total
        start += flat


def shifted_sum(p, members, start, taps):
    def tree(first, count):
        if count == 1:
            return p[first * members : (first + 1) * members, :]
        part = count // 2
        return tree(first, part) + roll_left(tree(first + part, part), part)

    return tree(start, taps)


def source_of(route):
    mask, other = route
    return lax.axis_index("tm") ^ jnp.where(lax.axis_index("span") == 0, mask, other)


def correlate(mask_ref, shards, routes, pieces_of_x, wide, ps, lead, local_taps, members, width, add_norm, add_sum):
    _, nblocks, _, rows = mask_ref.shape
    count = len(shards)
    pieces = 4
    blocks, taps = nblocks // pieces, local_taps // pieces

    def widen(n, c):
        spread(mask_ref, shards[n], wide[n % 2], range(c * blocks, (c + 1) * blocks))
        for raw_ref in shards[n]:
            squares = jnp.square(raw_ref[:, c * rows : (c + 1) * rows].astype(jnp.float32))
            add_norm(squares.reshape(-1, members, rows).sum(axis=0))

    def multiply(n, c):
        for start, samples in pieces_of_x[c::pieces]:
            value = samples()
            ps[n % 2][:, lead + start : lead + start + value.shape[1]] = jnp.dot(
                wide[n % 2][...], value, preferred_element_type=jnp.float32
            )

    def shift(n, c, total):
        lines = shifted_sum(ps[n % 2], members, c * taps, taps)
        if c > 0:
            lines = total + roll_left(lines, c * taps)
        if c < pieces - 1:
            return lines
        if lines.shape[1] < width:
            lines = jnp.concatenate([lines, jnp.zeros((members, width - lines.shape[1]), jnp.float32)], axis=1)
        add_sum(pltpu.roll(lines, (width + lead - local_taps * source_of(routes[n])) % width, axis=1))
        return None

    for c in range(pieces):
        widen(0, c)
    for n in range(count + 1):
        total = None
        for c in range(pieces):
            if n + 1 < count:
                widen(n + 1, c)
            if n > 0:
                total = shift(n - 1, c, total)
            if n < count:
                multiply(n, c)


def column_pieces(ref, start):
    size = min(2 * LANES, ref.shape[1])
    return [
        (start + low, lambda low=low: ref[:, low : low + size]) for low in range(0, ref.shape[1], size)
    ]


def absorb(masks, traces, shards, routes, carried, before, local_taps, tap_count):
    shards = [shard if isinstance(shard, list) else [shard] for shard in shards]
    lengths = [len(shard) for shard in shards]
    flat = sum(part.shape[0] for part in shards[0])
    members = flat // local_taps
    channels, lags = traces.shape
    half = tap_count // 2
    width = tap_count + lags

    def kernel(mask_ref, x_ref, *refs):
        inputs = []
        for length in lengths:
            inputs.append(refs[:length])
            refs = refs[length:]
        if carried is not None:
            old_sum, old_norm = refs[:2]
            refs = refs[2:]
        if before is not None:
            before_ref, main_ref, norm_ref, pre_ref, w0, w1, p0, p1, sums = refs
        else:
            sums, norm_ref, w0, w1, p0, p1 = refs
        for p in (p0, p1):
            p[:, :half] = jnp.zeros((flat, half), jnp.float32)
        if carried is None:
            sums[...] = jnp.zeros((members, width), jnp.float32)
            norm_ref[...] = jnp.zeros((members, LANES), jnp.float32)
        else:
            sums[...] = old_sum[...]
            norm_ref[...] = old_norm[...]

        def add_norm(value):
            norm_ref[...] += value

        def add_sum(value):
            sums[...] += value

        correlate(
            mask_ref, inputs, routes, column_pieces(x_ref, 0), (w0, w1), (p0, p1),
            half, local_taps, members, width, add_norm, add_sum,
        )
        if before is not None:
            main_ref[...] = sums[:, tap_count:]
            pre_ref[:members, :] = sums[:, :tap_count]
            pre_ref[members:, :] = before_ref[...]

    scratch = [pltpu.VMEM((flat, channels), jnp.bfloat16)] * 2 + [pltpu.VMEM((flat, half + lags), jnp.float32)] * 2
    norm_shape = pltpu.VMEM((members, LANES), jnp.float32)
    operands = [masks, traces] + [part for shard in shards for part in shard]
    if carried is not None:
        operands += list(carried)
    if before is not None:
        operands.append(before)
        scratch.append(pltpu.VMEM((members, width), jnp.float32))
        shapes = (pltpu.VMEM((members, lags), jnp.float32), norm_shape, pltpu.VMEM((2 * members, tap_count), jnp.float32))
    else:
        shapes = (pltpu.VMEM((members, width), jnp.float32), norm_shape)
    return pl.pallas_call(
        kernel,
        out_shape=shapes,
        in_specs=[VMEM] * len(operands),
        out_specs=(VMEM,) * len(shapes),
        scratch_shapes=scratch,
        compiler_params=PARAMS,
    )(*[resident(value) for value in operands])


def finish(main, norm, energy, after, scale_factor):
    members, lags = main.shape
    tap_count = after.shape[1]
    tail = lags - tap_count

    def kernel(main_ref, norm_ref, energy_ref, after_ref, out_ref):
        norms = jnp.sum(norm_ref[...], axis=1, keepdims=True)
        factor = lax.rsqrt(energy_ref[:, :tail] * norms + epsilon) * scale_factor
        out_ref[:, :tail] = main_ref[:, :tail] * factor
        factor = lax.rsqrt((energy_ref[:, tail:] + after_ref[members:, :]) * norms + epsilon) * scale_factor
        out_ref[:, tail:] = (main_ref[:, tail:] + after_ref[:members, :]) * factor

    return pl.pallas_call(
        kernel,
        out_shape=jax.ShapeDtypeStruct((members, lags), jnp.float32),
        in_specs=[VMEM] * 4,
        compiler_params=PARAMS,
        name="finish",
    )(resident(main), resident(norm), resident(energy), resident(after))


def per_device_chips(traces, templates, blocks):
    channels, _ = traces.shape
    local_taps, members, row_count = templates.shape
    block_rows = row_count // blocks.shape[1]
    nblocks = channels // block_rows
    spans = lax.axis_size("span")
    count = lax.axis_size("tm")
    tap_count = local_taps * count
    both = ("span", "tm")
    listing = blocks.T

    def send(value, target):
        route = []
        for s in range(spans):
            for i in range(count):
                to = target(s, i)
                if to is not None:
                    route.append((s * count + i, to[0] * count + to[1]))
        return lax.ppermute(value, both, route)

    def over_core(value):
        return send(value, lambda s, i: (s, i ^ 1))

    def over_x(value):
        return send(value, lambda s, i: (s, i ^ 2))

    def over_y(value):
        return send(value, lambda s, i: (s ^ 1, i))

    def over_z(value):
        return send(value, lambda s, i: (s, i ^ 4))

    own = templates.reshape(local_taps * members, row_count)
    part = own.shape[0] // 2
    own_route, own_x_route, near_route, near_x_route = (0, 0), (2, 2), (4, 4), (6, 6)
    far_route, far_x_route, far_y_route, far_xy_route = (8, 12), (10, 14), (12, 8), (14, 10)

    def pair(route):
        return [route, (route[0] ^ 1, route[1] ^ 1)]

    state = [None]

    def take(shards, routes, final=None):
        state[0] = absorb(masks, samples, shards, routes, state[0], final, local_taps, tap_count)
        return state[0]

    far = send(own, lambda s, i: (s, i ^ far_route[s]))
    own_x = over_x(own)
    near = over_z(own)
    core_own = over_core(own)
    before, energy, masks, samples, own_here = prepare(listing, traces, own, members, nblocks, tap_count)
    take([own_here, core_own], pair(own_route))
    core_own_x = over_core(own_x)
    near_x = over_z(own_x)
    take([own_x, core_own_x], pair(own_x_route))
    far_x = over_x(far)
    far_y = over_y(far)
    core_near = over_core(near)
    core_far = over_core(far)
    take([near, far], [near_route, far_route])
    take([core_near, core_far], [pair(near_route)[1], pair(far_route)[1]])
    core_near_x = over_core(near_x)
    take([near_x], [near_x_route])
    far_y_part = far_y[:part]
    far_xy_0 = over_x(far_y_part)
    far_x_part = far_x[part:]
    far_xy_1 = over_y(far_x_part)
    core_far_y = over_core(far_y)
    core_far_x = over_core(far_x)
    take([far_x, far_y, core_near_x], [far_x_route, far_y_route, pair(near_x_route)[1]])
    core_far_xy_0 = over_core(far_xy_0)
    core_far_xy_1 = over_core(far_xy_1)
    take([core_far_x, core_far_y], [pair(far_x_route)[1], pair(far_y_route)[1]])
    main, norm, pre = take([[far_xy_0, far_xy_1], [core_far_xy_0, core_far_xy_1]], pair(far_xy_route), before)
    after = send(pre, lambda s, i: (s, i - 1) if i > 0 else None)
    return finish(main, norm, energy, after, math.sqrt(tap_count * row_count))


def fits(mesh, traces, templates, blocks):
    spans, count = mesh.shape["span"], mesh.shape["tm"]
    taps, members, rows = templates.shape
    local_taps = taps // count
    lags = traces.shape[1] // (spans * count)
    block_rows = rows // blocks.shape[1]
    return (
        spans == 2
        and count == 16
        and members == 16
        and local_taps == 16
        and lags % 512 == 0
        and lags >= taps
        and block_rows % 128 == 0
        and traces.shape[0] // block_rows == 8
    )


def solution(mesh):
    def program(traces, templates, blocks):
        chips = fits(mesh, traces, templates, blocks)

        def body(*operands):
            return (per_device_chips if chips else per_device_general)(*operands)

        mapped = jax.shard_map(
            body,
            mesh=mesh,
            in_specs=(P(None, ("span", "tm")), P("tm", None, None), P()),
            out_specs=P(None, ("span", "tm")),
            check_vma=False,
        )
        return mapped(traces, templates, blocks)

    return program
```

profile of v0, /device:TPU:11, one launch (start us, length us, event | category | flops | bytes accessed | tf_op | source)
XLA Modules:
  0.0 55.2 jit_solution(6797780814029874168)
XLA Ops:
  0.0 0.3 collective-permute-start.9
  0.3 2.3 %collective-permute-start = (bf16[256,512]{1,0:T(8,128)(2,1)}, bf16[256,512]{1,0:T(8,128)(2,1)S(1)}, u32[]{:S(2)}, u32[]{:S(2)}) collective-permute-start(bf16[256,512]{1,0:T(8,128)(2,1)} %bitcast.3), channel_id=1, source_target_pairs={{0,8},{1,9},{2,10},{3,11},{4,12},{5,13},{6,14},{7,15},{8,0},{9,1},... | collective-permute-start | bytes 786440 | tf_op jit(solution)/shard_map/ppermute | solution.py:333
  2.6 0.2 collective-permute-start.12
  2.7 4.7 %collective-permute-done.9.refs_0_ = bf16[256,512]{1,0:T(8,128)(2,1)S(1)} collective-permute-done((bf16[256,512]{1,0:T(8,128)(2,1)}, bf16[256,512]{1,0:T(8,128)(2,1)S(1)}, u32[]{:S(2)}, u32[]{:S(2)}) %collective-permute-start.9) | collective-permute-done | bytes 262176 | tf_op jit(solution)/shard_map/ppermute | solution.py:333
  7.4 0.2 collective-permute-start.10
  7.6 6.9 %collective-permute-done.refs_1_ = bf16[256,512]{1,0:T(8,128)(2,1)S(1)} collective-permute-done((bf16[256,512]{1,0:T(8,128)(2,1)}, bf16[256,512]{1,0:T(8,128)(2,1)S(1)}, u32[]{:S(2)}, u32[]{:S(2)}) %collective-permute-start) | collective-permute-done | bytes 262176 | tf_op jit(solution)/shard_map/ppermute | solution.py:333
  14.5 0.2 collective-permute-start.1
  14.7 1.2 %collective-permute-start.3 = (bf16[256,512]{1,0:T(8,128)(2,1)S(1)}, bf16[256,512]{1,0:T(8,128)(2,1)S(1)}, u32[]{:S(2)}, u32[]{:S(2)}) collective-permute-start(bf16[256,512]{1,0:T(8,128)(2,1)S(1)} %collective-permute-done.refs_1_), channel_id=1, source_target_pairs={{0,2},{1,3},{2,0},{3,1},{4,6},{5,7},{6,4},{7,5},{8,10},{9,11},{10,... | collective-permute-start | bytes 786440 | tf_op jit(solution)/shard_map/ppermute | solution.py:333
  15.9 1.9 %collective-permute-start.16 = (bf16[256,512]{1,0:T(8,128)(2,1)}, bf16[256,512]{1,0:T(8,128)(2,1)S(1)}, u32[]{:S(2)}, u32[]{:S(2)}) collective-permute-start(bf16[256,512]{1,0:T(8,128)(2,1)} %bitcast.5), channel_id=1, source_target_pairs={{0,1},{1,0},{2,3},{3,2},{4,5},{5,4},{6,7},{7,6},{8,9},{9,8},{10,11... | collective-permute-start | bytes 786440 | tf_op jit(solution)/shard_map/ppermute | solution.py:333
  17.8 0.0 collective-permute-done.12.refs_0_
  17.8 0.0 collective-permute-start.15
  17.8 1.8 %collective-permute-done.10.refs_0_ = bf16[256,512]{1,0:T(8,128)(2,1)S(1)} collective-permute-done((bf16[256,512]{1,0:T(8,128)(2,1)S(1)}, bf16[256,512]{1,0:T(8,128)(2,1)S(1)}, u32[]{:S(2)}, u32[]{:S(2)}) %collective-permute-start.10) | collective-permute-done | bytes 262176 | tf_op jit(solution)/shard_map/ppermute | solution.py:333
  19.7 1.8 %collective-permute-start.14 = (bf16[256,512]{1,0:T(8,128)(2,1)S(1)}, bf16[256,512]{1,0:T(8,128)(2,1)S(1)}, u32[]{:S(2)}, u32[]{:S(2)}) collective-permute-start(bf16[256,512]{1,0:T(8,128)(2,1)S(1)} %collective-permute-done.refs_1_), channel_id=1, source_target_pairs={{0,1},{1,0},{2,3},{3,2},{4,5},{5,4},{6,7},{7,6},{8,9},{9,8},{10,11... | collective-permute-start | bytes 786440 | tf_op jit(solution)/shard_map/ppermute | solution.py:333
  21.5 0.3 collective-permute-done.1.refs_1_
  21.8 1.3 %collective-permute-start.13 = (bf16[256,512]{1,0:T(8,128)(2,1)S(1)}, bf16[256,512]{1,0:T(8,128)(2,1)S(1)}, u32[]{:S(2)}, u32[]{:S(2)}) collective-permute-start(bf16[256,512]{1,0:T(8,128)(2,1)S(1)} %collective-permute-done.12.refs_0_), channel_id=1, source_target_pairs={{0,1},{1,0},{2,3},{3,2},{4,5},{5,4},{6,7},{7,6},{8,9},{9,8},{10,11... | collective-permute-start | bytes 786440 | tf_op jit(solution)/shard_map/ppermute | solution.py:333
  23.2 0.0 collective-permute-done.3.refs_0_
  23.2 0.2 collective-permute-start.11
  23.4 0.0 collective-permute-done.16.refs_1_
  23.4 0.5 collective-permute-start.7
  23.9 0.0 collective-permute-done.15.refs_1_
  23.9 0.1 collective-permute-start.8
  24.0 0.0 collective-permute-done.14.refs_1_
  24.0 1.2 %collective-permute-start.2 = (bf16[128,512]{1,0:T(8,128)(2,1)S(1)}, bf16[128,512]{1,0:T(8,128)(2,1)S(1)}, u32[]{:S(2)}, u32[]{:S(2)}) collective-permute-start(bf16[128,512]{1,0:T(8,128)(2,1)S(1)} %slice.8), channel_id=1, source_target_pairs={{0,2},{1,3},{2,0},{3,1},{4,6},{5,7},{6,4},{7,5},{8,10},{9,11},{10,... | collective-permute-start | bytes 393224 | tf_op jit(solution)/shard_map/ppermute | solution.py:333
  25.2 0.0 collective-permute-done.13.refs_0_
  25.2 1.3 %collective-permute-start.4 = (bf16[128,512]{1,0:T(8,128)(2,1)S(1)}, bf16[128,512]{1,0:T(8,128)(2,1)S(1)}, u32[]{:S(2)}, u32[]{:S(2)}) collective-permute-start(bf16[128,512]{1,0:T(8,128)(2,1)S(1)} %slice.9), channel_id=1, source_target_pairs={{0,16},{1,17},{2,18},{3,19},{4,20},{5,21},{6,22},{7,23},{8,24},{9,... | collective-permute-start | bytes 393224 | tf_op jit(solution)/shard_map/ppermute | solution.py:333
  26.5 2.2 %collective-permute-done.2.refs_0_ = bf16[128,512]{1,0:T(8,128)(2,1)S(1)} collective-permute-done((bf16[128,512]{1,0:T(8,128)(2,1)S(1)}, bf16[128,512]{1,0:T(8,128)(2,1)S(1)}, u32[]{:S(2)}, u32[]{:S(2)}) %collective-permute-start.2) | collective-permute-done | bytes 131104 | tf_op jit(solution)/shard_map/ppermute | solution.py:333
  28.7 1.2 %collective-permute-start.5 = (bf16[128,512]{1,0:T(8,128)(2,1)S(1)}, bf16[128,512]{1,0:T(8,128)(2,1)S(1)}, u32[]{:S(2)}, u32[]{:S(2)}) collective-permute-start(bf16[128,512]{1,0:T(8,128)(2,1)S(1)} %collective-permute-done.2.refs_0_), channel_id=1, source_target_pairs={{0,1},{1,0},{2,3},{3,2},{4,5},{5,4},{6,7},{7,6},{8,9},{9,8},{10,11... | collective-permute-start | bytes 393224 | tf_op jit(solution)/shard_map/ppermute | solution.py:333
  29.9 0.0 collective-permute-done.4.refs_1_
  29.9 1.2 %collective-permute-start.6 = (bf16[128,512]{1,0:T(8,128)(2,1)S(1)}, bf16[128,512]{1,0:T(8,128)(2,1)S(1)}, u32[]{:S(2)}, u32[]{:S(2)}) collective-permute-start(bf16[128,512]{1,0:T(8,128)(2,1)S(1)} %collective-permute-done.4.refs_1_), channel_id=1, source_target_pairs={{0,1},{1,0},{2,3},{3,2},{4,5},{5,4},{6,7},{7,6},{8,9},{9,8},{10,11... | collective-permute-start | bytes 393224 | tf_op jit(solution)/shard_map/ppermute | solution.py:333
  31.1 2.9 %prepare.1 = (f32[16,256]{1,0:T(8,128)S(1)}, f32[16,1024]{1,0:T(8,128)S(1)}, bf16[4,8,16,128]{3,2,1,0:T(8,128)(2,1)S(1)}, bf16[1024,1024]{1,0:T(8,128)(2,1)S(1)}, bf16[256,512]{1,0:T(8,128)(2,1)S(1)}) custom-call(s32[4,16]{1,0:T(4,128)} %bitcast.7, bf16[1024,1024]{1,0:T(8,128)(2,1)} %x_hbm.1, bf16[256,512]{1,0:T(8,128)(2,1)} %bitcast.6), custom_call_target="tpu_custom_call" | custom-call | tf_op jit(solution)/shard_map/prepare/pallas_call | solution.py:131
  34.0 1.7 %shard_map.37 = (f32[16,1280]{1,0:T(8,128)S(1)}, f32[16,128]{1,0:T(8,128)S(1)}) custom-call(bf16[4,8,16,128]{3,2,1,0:T(8,128)(2,1)S(1)} %get-tuple-element.27.mask_ref, bf16[1024,1024]{1,0:T(8,128)(2,1)S(1)} %get-tuple-element.28.x_ref, bf16[256,512]{1,0:T(8,128)(2,1)S(1)} %get-tuple-element.29.refs_0_, bf16[256,512]{1,0:T(8,128)(2,1)S(1)} %collective-permute-done.16.refs_1_), custom_call_target="tpu_custom_call" | custom-call | tf_op jit(solution)/shard_map/pallas_call | solution.py:284
  35.8 1.8 %shard_map.38 = (f32[16,1280]{1,0:T(8,128)S(1)}, f32[16,128]{1,0:T(8,128)S(1)}) custom-call(bf16[4,8,16,128]{3,2,1,0:T(8,128)(2,1)S(1)} %get-tuple-element.27.mask_ref, bf16[1024,1024]{1,0:T(8,128)(2,1)S(1)} %get-tuple-element.28.x_ref, bf16[256,512]{1,0:T(8,128)(2,1)S(1)} %collective-permute-done.9.refs_0_, ...), custom_call_target="tpu_custom_call" | custom-call | tf_op jit(solution)/shard_map/pallas_call | solution.py:284
  37.6 1.8 %shard_map.39 = (f32[16,1280]{1,0:T(8,128)S(1)}, f32[16,128]{1,0:T(8,128)S(1)}) custom-call(bf16[4,8,16,128]{3,2,1,0:T(8,128)(2,1)S(1)} %get-tuple-element.27.mask_ref, bf16[1024,1024]{1,0:T(8,128)(2,1)S(1)} %get-tuple-element.28.x_ref, bf16[256,512]{1,0:T(8,128)(2,1)S(1)} %collective-permute-done.12.refs_0_, ...), custom_call_target="tpu_custom_call" | custom-call | tf_op jit(solution)/shard_map/pallas_call | solution.py:284
  39.3 1.8 %shard_map.40 = (f32[16,1280]{1,0:T(8,128)S(1)}, f32[16,128]{1,0:T(8,128)S(1)}) custom-call(bf16[4,8,16,128]{3,2,1,0:T(8,128)(2,1)S(1)} %get-tuple-element.27.mask_ref, bf16[1024,1024]{1,0:T(8,128)(2,1)S(1)} %get-tuple-element.28.x_ref, bf16[256,512]{1,0:T(8,128)(2,1)S(1)} %collective-permute-done.13.refs_0_, ...), custom_call_target="tpu_custom_call" | custom-call | tf_op jit(solution)/shard_map/pallas_call | solution.py:284
  41.1 1.1 %shard_map.41 = (f32[16,1280]{1,0:T(8,128)S(1)}, f32[16,128]{1,0:T(8,128)S(1)}) custom-call(bf16[4,8,16,128]{3,2,1,0:T(8,128)(2,1)S(1)} %get-tuple-element.27.mask_ref, bf16[1024,1024]{1,0:T(8,128)(2,1)S(1)} %get-tuple-element.28.x_ref, bf16[256,512]{1,0:T(8,128)(2,1)S(1)} %collective-permute-done.10.refs_0_, f32[16,1280]{1,0:T(8,128)S(1)} %get-tuple-element.36.refs_1_, ...), custom_call_target="tpu_custom_call" | custom-call | tf_op jit(solution)/shard_map/pallas_call | solution.py:284
  42.2 0.0 collective-permute-done.11.refs_2_
  42.2 2.4 %shard_map.42 = (f32[16,1280]{1,0:T(8,128)S(1)}, f32[16,128]{1,0:T(8,128)S(1)}) custom-call(bf16[4,8,16,128]{3,2,1,0:T(8,128)(2,1)S(1)} %get-tuple-element.27.mask_ref, bf16[1024,1024]{1,0:T(8,128)(2,1)S(1)} %get-tuple-element.28.x_ref, bf16[256,512]{1,0:T(8,128)(2,1)S(1)} %collective-permute-done.3.refs_0_, ...), custom_call_target="tpu_custom_call" | custom-call | tf_op jit(solution)/shard_map/pallas_call | solution.py:284
  44.6 0.0 collective-permute-done.7.refs_0_
  44.7 0.0 collective-permute-done.8.refs_1_
  44.7 1.8 %shard_map.43 = (f32[16,1280]{1,0:T(8,128)S(1)}, f32[16,128]{1,0:T(8,128)S(1)}) custom-call(bf16[4,8,16,128]{3,2,1,0:T(8,128)(2,1)S(1)} %get-tuple-element.27.mask_ref, bf16[1024,1024]{1,0:T(8,128)(2,1)S(1)} %get-tuple-element.28.x_ref, bf16[256,512]{1,0:T(8,128)(2,1)S(1)} %collective-permute-done.7.refs_0_, ...), custom_call_target="tpu_custom_call" | custom-call | tf_op jit(solution)/shard_map/pallas_call | solution.py:284
  46.4 0.0 collective-permute-done.5.refs_2_
  46.4 0.0 collective-permute-done.6.refs_3_
  46.5 1.8 %shard_map.44 = (f32[16,1024]{1,0:T(8,128)S(1)}, f32[16,128]{1,0:T(8,128)S(1)}, f32[32,256]{1,0:T(8,128)S(1)}) custom-call(bf16[4,8,16,128]{3,2,1,0:T(8,128)(2,1)S(1)} %get-tuple-element.27.mask_ref, bf16[1024,1024]{1,0:T(8,128)(2,1)S(1)} %get-tuple-element.28.x_ref, bf16[128,512]{1,0:T(8,128)(2,1)S(1)} %collective-permute-done.2.refs_0_, ...), custom_call_target="tpu_custom_call" | custom-call | tf_op jit(solution)/shard_map/pallas_call | solution.py:284
  48.3 1.9 %collective-permute-start.17 = (f32[32,256]{1,0:T(8,128)S(1)}, f32[32,256]{1,0:T(8,128)S(1)}, u32[]{:S(2)}, u32[]{:S(2)}) collective-permute-start(f32[32,256]{1,0:T(8,128)S(1)} %get-tuple-element.48), channel_id=1, source_target_pairs={{1,0},{2,1},{3,2},{4,3},{5,4},{6,5},{7,6},{8,7},{9,8},{10,9},{11,1... | collective-permute-start | bytes 98312 | tf_op jit(solution)/shard_map/ppermute | solution.py:333
  50.2 4.2 %collective-permute-done.17.after_ref = f32[32,256]{1,0:T(8,128)S(1)} collective-permute-done((f32[32,256]{1,0:T(8,128)S(1)}, f32[32,256]{1,0:T(8,128)S(1)}, u32[]{:S(2)}, u32[]{:S(2)}) %collective-permute-start.17) | collective-permute-done | bytes 32800 | tf_op jit(solution)/shard_map/ppermute | solution.py:333
  54.4 0.7 %finish.1 = f32[16,1024]{1,0:T(8,128)} custom-call(f32[16,1024]{1,0:T(8,128)S(1)} %get-tuple-element.45.main_ref, f32[16,128]{1,0:T(8,128)S(1)} %get-tuple-element.46.norm_ref, f32[16,1024]{1,0:T(8,128)S(1)} %get-tuple-element.47.energy_ref, f32[32,256]{1,0:T(8,128)S(1)} %collective-permute-done.17.after_ref), custom_call_target="tpu_custom_call" | custom-call | tf_op jit(solution)/shard_map/finish/pallas_call | solution.py:306
  (2 shorter events, 0.0 us)
Async XLA Ops:
  0.0 7.4 %collective-permute-start.9 = (bf16[256,512]{1,0:T(8,128)(2,1)}, bf16[256,512]{1,0:T(8,128)(2,1)S(1)}, u32[]{:S(2)}, u32[]{:S(2)}) collective-permute-start(bf16[256,512]{1,0:T(8,128)(2,1)} %bitcast.2), channel_id=1, source_target_pairs={{0,2},{1,3},{2,0},{3,1},{4,6},{5,7},{6,4},{7,5},{8,10},{9,11},{10,... | collective-permute-start | bytes 786440 | tf_op jit(solution)/shard_map/ppermute | solution.py:333
  0.3 14.2 %collective-permute-start = (bf16[256,512]{1,0:T(8,128)(2,1)}, bf16[256,512]{1,0:T(8,128)(2,1)S(1)}, u32[]{:S(2)}, u32[]{:S(2)}) collective-permute-start(bf16[256,512]{1,0:T(8,128)(2,1)} %bitcast.3), channel_id=1, source_target_pairs={{0,8},{1,9},{2,10},{3,11},{4,12},{5,13},{6,14},{7,15},{8,0},{9,1},... | collective-permute-start | bytes 786440 | tf_op jit(solution)/shard_map/ppermute | solution.py:333
  2.6 15.3 %collective-permute-start.12 = (bf16[256,512]{1,0:T(8,128)(2,1)}, bf16[256,512]{1,0:T(8,128)(2,1)S(1)}, u32[]{:S(2)}, u32[]{:S(2)}) collective-permute-start(bf16[256,512]{1,0:T(8,128)(2,1)} %bitcast.4), channel_id=1, source_target_pairs={{0,4},{1,5},{2,6},{3,7},{4,0},{5,1},{6,2},{7,3},{8,12},{9,13},{10,... | collective-permute-start | bytes 786440 | tf_op jit(solution)/shard_map/ppermute | solution.py:333
  7.4 12.3 %collective-permute-start.10 = (bf16[256,512]{1,0:T(8,128)(2,1)S(1)}, bf16[256,512]{1,0:T(8,128)(2,1)S(1)}, u32[]{:S(2)}, u32[]{:S(2)}) collective-permute-start(bf16[256,512]{1,0:T(8,128)(2,1)S(1)} %collective-permute-done.9.refs_0_), channel_id=1, source_target_pairs={{0,4},{1,5},{2,6},{3,7},{4,0},{5,1},{6,2},{7,3},{8,12},{9,13},{10,... | collective-permute-start | bytes 786440 | tf_op jit(solution)/shard_map/ppermute | solution.py:333
  14.5 7.4 %collective-permute-start.1 = (bf16[256,512]{1,0:T(8,128)(2,1)S(1)}, bf16[256,512]{1,0:T(8,128)(2,1)S(1)}, u32[]{:S(2)}, u32[]{:S(2)}) collective-permute-start(bf16[256,512]{1,0:T(8,128)(2,1)S(1)} %collective-permute-done.refs_1_), channel_id=1, source_target_pairs={{0,16},{1,17},{2,18},{3,19},{4,20},{5,21},{6,22},{7,23},{8,24},{9,... | collective-permute-start | bytes 786440 | tf_op jit(solution)/shard_map/ppermute | solution.py:333
  14.7 8.5 %collective-permute-start.3 = (bf16[256,512]{1,0:T(8,128)(2,1)S(1)}, bf16[256,512]{1,0:T(8,128)(2,1)S(1)}, u32[]{:S(2)}, u32[]{:S(2)}) collective-permute-start(bf16[256,512]{1,0:T(8,128)(2,1)S(1)} %collective-permute-done.refs_1_), channel_id=1, source_target_pairs={{0,2},{1,3},{2,0},{3,1},{4,6},{5,7},{6,4},{7,5},{8,10},{9,11},{10,... | collective-permute-start | bytes 786440 | tf_op jit(solution)/shard_map/ppermute | solution.py:333
  15.9 7.5 %collective-permute-start.16 = (bf16[256,512]{1,0:T(8,128)(2,1)}, bf16[256,512]{1,0:T(8,128)(2,1)S(1)}, u32[]{:S(2)}, u32[]{:S(2)}) collective-permute-start(bf16[256,512]{1,0:T(8,128)(2,1)} %bitcast.5), channel_id=1, source_target_pairs={{0,1},{1,0},{2,3},{3,2},{4,5},{5,4},{6,7},{7,6},{8,9},{9,8},{10,11... | collective-permute-start | bytes 786440 | tf_op jit(solution)/shard_map/ppermute | solution.py:333
  17.8 6.0 %collective-permute-start.15 = (bf16[256,512]{1,0:T(8,128)(2,1)S(1)}, bf16[256,512]{1,0:T(8,128)(2,1)S(1)}, u32[]{:S(2)}, u32[]{:S(2)}) collective-permute-start(bf16[256,512]{1,0:T(8,128)(2,1)S(1)} %collective-permute-done.9.refs_0_), channel_id=1, source_target_pairs={{0,1},{1,0},{2,3},{3,2},{4,5},{5,4},{6,7},{7,6},{8,9},{9,8},{10,11... | collective-permute-start | bytes 786440 | tf_op jit(solution)/shard_map/ppermute | solution.py:333
  19.7 4.3 %collective-permute-start.14 = (bf16[256,512]{1,0:T(8,128)(2,1)S(1)}, bf16[256,512]{1,0:T(8,128)(2,1)S(1)}, u32[]{:S(2)}, u32[]{:S(2)}) collective-permute-start(bf16[256,512]{1,0:T(8,128)(2,1)S(1)} %collective-permute-done.refs_1_), channel_id=1, source_target_pairs={{0,1},{1,0},{2,3},{3,2},{4,5},{5,4},{6,7},{7,6},{8,9},{9,8},{10,11... | collective-permute-start | bytes 786440 | tf_op jit(solution)/shard_map/ppermute | solution.py:333
  21.8 3.4 %collective-permute-start.13 = (bf16[256,512]{1,0:T(8,128)(2,1)S(1)}, bf16[256,512]{1,0:T(8,128)(2,1)S(1)}, u32[]{:S(2)}, u32[]{:S(2)}) collective-permute-start(bf16[256,512]{1,0:T(8,128)(2,1)S(1)} %collective-permute-done.12.refs_0_), channel_id=1, source_target_pairs={{0,1},{1,0},{2,3},{3,2},{4,5},{5,4},{6,7},{7,6},{8,9},{9,8},{10,11... | collective-permute-start | bytes 786440 | tf_op jit(solution)/shard_map/ppermute | solution.py:333
  23.2 19.0 %collective-permute-start.11 = (bf16[256,512]{1,0:T(8,128)(2,1)S(1)}, bf16[256,512]{1,0:T(8,128)(2,1)S(1)}, u32[]{:S(2)}, u32[]{:S(2)}) collective-permute-start(bf16[256,512]{1,0:T(8,128)(2,1)S(1)} %collective-permute-done.10.refs_0_), channel_id=1, source_target_pairs={{0,1},{1,0},{2,3},{3,2},{4,5},{5,4},{6,7},{7,6},{8,9},{9,8},{10,11... | collective-permute-start | bytes 786440 | tf_op jit(solution)/shard_map/ppermute | solution.py:333
  23.4 21.2 %collective-permute-start.7 = (bf16[256,512]{1,0:T(8,128)(2,1)S(1)}, bf16[256,512]{1,0:T(8,128)(2,1)S(1)}, u32[]{:S(2)}, u32[]{:S(2)}) collective-permute-start(bf16[256,512]{1,0:T(8,128)(2,1)S(1)} %collective-permute-done.3.refs_0_), channel_id=1, source_target_pairs={{0,1},{1,0},{2,3},{3,2},{4,5},{5,4},{6,7},{7,6},{8,9},{9,8},{10,11... | collective-permute-start | bytes 786440 | tf_op jit(solution)/shard_map/ppermute | solution.py:333
  23.9 20.8 %collective-permute-start.8 = (bf16[256,512]{1,0:T(8,128)(2,1)S(1)}, bf16[256,512]{1,0:T(8,128)(2,1)S(1)}, u32[]{:S(2)}, u32[]{:S(2)}) collective-permute-start(bf16[256,512]{1,0:T(8,128)(2,1)S(1)} %collective-permute-done.1.refs_1_), channel_id=1, source_target_pairs={{0,1},{1,0},{2,3},{3,2},{4,5},{5,4},{6,7},{7,6},{8,9},{9,8},{10,11... | collective-permute-start | bytes 786440 | tf_op jit(solution)/shard_map/ppermute | solution.py:333
  24.0 4.7 %collective-permute-start.2 = (bf16[128,512]{1,0:T(8,128)(2,1)S(1)}, bf16[128,512]{1,0:T(8,128)(2,1)S(1)}, u32[]{:S(2)}, u32[]{:S(2)}) collective-permute-start(bf16[128,512]{1,0:T(8,128)(2,1)S(1)} %slice.8), channel_id=1, source_target_pairs={{0,2},{1,3},{2,0},{3,1},{4,6},{5,7},{6,4},{7,5},{8,10},{9,11},{10,... | collective-permute-start | bytes 393224 | tf_op jit(solution)/shard_map/ppermute | solution.py:333
  25.2 4.7 %collective-permute-start.4 = (bf16[128,512]{1,0:T(8,128)(2,1)S(1)}, bf16[128,512]{1,0:T(8,128)(2,1)S(1)}, u32[]{:S(2)}, u32[]{:S(2)}) collective-permute-start(bf16[128,512]{1,0:T(8,128)(2,1)S(1)} %slice.9), channel_id=1, source_target_pairs={{0,16},{1,17},{2,18},{3,19},{4,20},{5,21},{6,22},{7,23},{8,24},{9,... | collective-permute-start | bytes 393224 | tf_op jit(solution)/shard_map/ppermute | solution.py:333
  28.7 17.8 %collective-permute-start.5 = (bf16[128,512]{1,0:T(8,128)(2,1)S(1)}, bf16[128,512]{1,0:T(8,128)(2,1)S(1)}, u32[]{:S(2)}, u32[]{:S(2)}) collective-permute-start(bf16[128,512]{1,0:T(8,128)(2,1)S(1)} %collective-permute-done.2.refs_0_), channel_id=1, source_target_pairs={{0,1},{1,0},{2,3},{3,2},{4,5},{5,4},{6,7},{7,6},{8,9},{9,8},{10,11... | collective-permute-start | bytes 393224 | tf_op jit(solution)/shard_map/ppermute | solution.py:333
  29.9 16.5 %collective-permute-start.6 = (bf16[128,512]{1,0:T(8,128)(2,1)S(1)}, bf16[128,512]{1,0:T(8,128)(2,1)S(1)}, u32[]{:S(2)}, u32[]{:S(2)}) collective-permute-start(bf16[128,512]{1,0:T(8,128)(2,1)S(1)} %collective-permute-done.4.refs_1_), channel_id=1, source_target_pairs={{0,1},{1,0},{2,3},{3,2},{4,5},{5,4},{6,7},{7,6},{8,9},{9,8},{10,11... | collective-permute-start | bytes 393224 | tf_op jit(solution)/shard_map/ppermute | solution.py:333
  48.3 6.1 %collective-permute-start.17 = (f32[32,256]{1,0:T(8,128)S(1)}, f32[32,256]{1,0:T(8,128)S(1)}, u32[]{:S(2)}, u32[]{:S(2)}) collective-permute-start(f32[32,256]{1,0:T(8,128)S(1)} %get-tuple-element.48), channel_id=1, source_target_pairs={{1,0},{2,1},{3,2},{4,3},{5,4},{6,5},{7,6},{8,7},{9,8},{10,9},{11,1... | collective-permute-start | bytes 98312 | tf_op jit(solution)/shard_map/ppermute | solution.py:333
where the time goes:
time: 55.4 us; the launch traced here: 55.2 us
  waiting for transfers between devices  20.2 us (36%)
  Pallas kernels  17.8 us (32%)
  starting transfers between devices  17 us (31%)
    ppermute x18, waiting for transfers between devices, send(): return lax.ppermute(value, both, route)  20.2 us
    ppermute x18, starting transfers between devices, send(): return lax.ppermute(value, both, route)  17 us
    pallas_call x8, Pallas kernels, absorb(): pl.pallas_call(kernel, out_shape=shapes, in_specs=[VMEM] * len(operands),...  14.1 us
    pallas_call x1, Pallas kernels, prepare(): pl.pallas_call(kernel, out_shape=(pltpu.VMEM((members, tap_count), jnp.fl...  2.92 us
  transfers between devices with their start and end apart: 18, of which 6 were waited for; matrix products, arithmetic and copies ran while one was open for 0% of the time, Pallas kernels for 28%

commit v1 on v0

--- a/solution.py
+++ b/solution.py
@@ -151,12 +151,12 @@
     for raw_ref in raw_refs:
         flat = raw_ref.shape[0]
         for n in blocks:
-            total = jnp.zeros((flat, rows), jnp.bfloat16)
-            for m in range(listed):
-                mask = (mask_ref[m, n] > 0)[None]
-                mask = jnp.broadcast_to(mask, (flat // members, members, rows)).reshape(flat, rows)
-                total = jnp.where(mask, raw_ref[:, m * rows : (m + 1) * rows], total)
-            wide[start : start + flat, n * rows : (n + 1) * rows] = total
+            tests = [mask_ref[m, n] > 0 for m in range(listed)]
+            for t in range(0, flat, members):
+                total = jnp.zeros((members, rows), jnp.bfloat16)
+                for m in range(listed):
+                    total = jnp.where(tests[m], raw_ref[t : t + members, m * rows : (m + 1) * rows], total)
+                wide[start + t : start + t + members, n * rows : (n + 1) * rows] = total
         start += flat
 
 
@@ -175,64 +175,24 @@
     return lax.axis_index("tm") ^ jnp.where(lax.axis_index("span") == 0, mask, other)
 
 
-def correlate(mask_ref, shards, routes, pieces_of_x, wide, ps, lead, local_taps, members, width, add_norm, add_sum):
-    _, nblocks, _, rows = mask_ref.shape
-    count = len(shards)
-    pieces = 4
-    blocks, taps = nblocks // pieces, local_taps // pieces
-
-    def widen(n, c):
-        spread(mask_ref, shards[n], wide[n % 2], range(c * blocks, (c + 1) * blocks))
-        for raw_ref in shards[n]:
-            squares = jnp.square(raw_ref[:, c * rows : (c + 1) * rows].astype(jnp.float32))
-            add_norm(squares.reshape(-1, members, rows).sum(axis=0))
-
-    def multiply(n, c):
-        for start, samples in pieces_of_x[c::pieces]:
-            value = samples()
-            ps[n % 2][:, lead + start : lead + start + value.shape[1]] = jnp.dot(
-                wide[n % 2][...], value, preferred_element_type=jnp.float32
-            )
-
-    def shift(n, c, total):
-        lines = shifted_sum(ps[n % 2], members, c * taps, taps)
-        if c > 0:
-            lines = total + roll_left(lines, c * taps)
-        if c < pieces - 1:
-            return lines
-        if lines.shape[1] < width:
-            lines = jnp.concatenate([lines, jnp.zeros((members, width - lines.shape[1]), jnp.float32)], axis=1)
-        add_sum(pltpu.roll(lines, (width + lead - local_taps * source_of(routes[n])) % width, axis=1))
-        return None
-
-    for c in range(pieces):
-        widen(0, c)
-    for n in range(count + 1):
-        total = None
-        for c in range(pieces):
-            if n + 1 < count:
-                widen(n + 1, c)
-            if n > 0:
-                total = shift(n - 1, c, total)
-            if n < count:
-                multiply(n, c)
-
-
-def column_pieces(ref, start):
-    size = min(2 * LANES, ref.shape[1])
-    return [
-        (start + low, lambda low=low: ref[:, low : low + size]) for low in range(0, ref.shape[1], size)
-    ]
-
-
-def absorb(masks, traces, shards, routes, carried, before, local_taps, tap_count):
+def column_pieces(width):
+    size = min(2 * LANES, width)
+    return [(low, size) for low in range(0, width, size)]
+
+
+def absorb(masks, traces, shards, routes, carried, local_taps, tap_count):
     shards = [shard if isinstance(shard, list) else [shard] for shard in shards]
     lengths = [len(shard) for shard in shards]
-    flat = sum(part.shape[0] for part in shards[0])
+    flat, rows = sum(part.shape[0] for part in shards[0]), shards[0][0].shape[1]
     members = flat // local_taps
     channels, lags = traces.shape
     half = tap_count // 2
     width = tap_count + lags
+    count = len(shards)
+    nblocks = masks.shape[1]
+    pieces = 4
+    blocks, taps = nblocks // pieces, local_taps // pieces
+    pending = [] if carried is None else [carried[3]]
 
     def kernel(mask_ref, x_ref, *refs):
         inputs = []
@@ -240,13 +200,12 @@
             inputs.append(refs[:length])
             refs = refs[length:]
         if carried is not None:
-            old_sum, old_norm = refs[:2]
-            refs = refs[2:]
-        if before is not None:
-            before_ref, main_ref, norm_ref, pre_ref, w0, w1, p0, p1, sums = refs
-        else:
-            sums, norm_ref, w0, w1, p0, p1 = refs
-        for p in (p0, p1):
+            old_sum, old_norm, old_p = refs[:3]
+            refs = refs[3:]
+        sums, norm_ref, out_p, w0, w1, p0, p1 = refs
+        wide, ps = (w0, w1), [(p0, p1)[n % 2] for n in range(count)]
+        ps[-1] = out_p
+        for p in ps[-2:]:
             p[:, :half] = jnp.zeros((flat, half), jnp.float32)
         if carried is None:
             sums[...] = jnp.zeros((members, width), jnp.float32)
@@ -254,40 +213,163 @@
         else:
             sums[...] = old_sum[...]
             norm_ref[...] = old_norm[...]
-
-        def add_norm(value):
-            norm_ref[...] += value
-
-        def add_sum(value):
-            sums[...] += value
-
-        correlate(
-            mask_ref, inputs, routes, column_pieces(x_ref, 0), (w0, w1), (p0, p1),
-            half, local_taps, members, width, add_norm, add_sum,
-        )
-        if before is not None:
-            main_ref[...] = sums[:, tap_count:]
-            pre_ref[:members, :] = sums[:, :tap_count]
-            pre_ref[members:, :] = before_ref[...]
-
-    scratch = [pltpu.VMEM((flat, channels), jnp.bfloat16)] * 2 + [pltpu.VMEM((flat, half + lags), jnp.float32)] * 2
+        for p in ps[:-2]:
+            p[:, :half] = jnp.zeros((flat, half), jnp.float32)
+        waiting = [(old_p, route) for route in pending] + list(zip(ps, routes))
+
+        def widen(n, c):
+            spread(mask_ref, inputs[n], wide[n % 2], range(c * blocks, (c + 1) * blocks))
+
+        def measure(n, c):
+            for raw_ref in inputs[n]:
+                part = raw_ref[:, c * rows // pieces : (c + 1) * rows // pieces]
+                squares = jnp.square(part.astype(jnp.float32))
+                norm_ref[...] += squares.reshape(-1, members, rows // pieces).sum(axis=0)
+
+        def multiply(n, c):
+            for start, size in column_pieces(lags)[c::pieces]:
+                ps[n][:, half + start : half + start + size] = jnp.dot(
+                    wide[n % 2][...], x_ref[:, start : start + size], preferred_element_type=jnp.float32
+                )
+
+        def shift(entry, c, total):
+            p, route = entry
+            lines = shifted_sum(p, members, c * taps, taps)
+            if c > 0:
+                lines = total + roll_left(lines, c * taps)
+            if c < pieces - 1:
+                return lines
+            lines = jnp.concatenate([lines, jnp.zeros((members, tap_count - half), jnp.float32)], axis=1)
+            distance = (width + half - local_taps * source_of(route)) % width
+            sums[...] += pltpu.roll(lines, distance, axis=1)
+            return None
+
+        late = len(pending)
+        for c in range(pieces):
+            widen(0, c)
+        for n in range(count):
+            entry = n - 1 + late
+            total = None
+            for c in range(pieces):
+                if n + 1 < count:
+                    widen(n + 1, c)
+                if entry >= 0:
+                    total = shift(waiting[entry], c, total)
+                multiply(n, c)
+                if n == count - 1:
+                    for m in range(count):
+                        measure(m, c)
+
+    product_shape = pltpu.VMEM((flat, half + lags), jnp.float32)
+    scratch = [pltpu.VMEM((flat, channels), jnp.bfloat16)] * 2 + [product_shape] * 2
     norm_shape = pltpu.VMEM((members, LANES), jnp.float32)
     operands = [masks, traces] + [part for shard in shards for part in shard]
     if carried is not None:
-        operands += list(carried)
-    if before is not None:
-        operands.append(before)
-        scratch.append(pltpu.VMEM((members, width), jnp.float32))
-        shapes = (pltpu.VMEM((members, lags), jnp.float32), norm_shape, pltpu.VMEM((2 * members, tap_count), jnp.float32))
-    else:
-        shapes = (pltpu.VMEM((members, width), jnp.float32), norm_shape)
-    return pl.pallas_call(
+        operands += carried[:3]
+    shapes = (pltpu.VMEM((members, width), jnp.float32), norm_shape, product_shape)
+    results = pl.pallas_call(
         kernel,
         out_shape=shapes,
         in_specs=[VMEM] * len(operands),
         out_specs=(VMEM,) * len(shapes),
         scratch_shapes=scratch,
         compiler_params=PARAMS,
+    )(*[resident(value) for value in operands])
+    return [*results, routes[-1]]
+
+
+def place_lines(lines, route, local_taps, tap_count, width):
+    members, have = lines.shape
+    lines = jnp.concatenate([lines, jnp.zeros((members, width - have), jnp.float32)], axis=1)
+    return pltpu.roll(lines, (width + tap_count // 2 - local_taps * source_of(route)) % width, axis=1)
+
+
+def edge(masks, traces, shards, routes, carried, before, local_taps, tap_count):
+    sums, norm, products, route = carried
+    flat, rows = sum(part.shape[0] for part in shards[0]), shards[0][0].shape[1]
+    members, width = sums.shape
+    channels, lags = traces.shape
+    half = tap_count // 2
+    count = len(shards)
+    nblocks = masks.shape[1]
+    lengths = [len(shard) for shard in shards]
+
+    def kernel(mask_ref, x_ref, old_sum, old_norm, p_ref, before_ref, *refs):
+        inputs = []
+        for length in lengths:
+            inputs.append(refs[:length])
+            refs = refs[length:]
+        pre_ref, main_ref, norm_ref = refs[:3]
+        wide, ps = refs[3 : 3 + count], refs[3 + count :]
+        for p in ps:
+            p[:, :half] = jnp.zeros((flat, half), jnp.float32)
+        norms = old_norm[...]
+        for n in range(count):
+            spread(mask_ref, inputs[n], wide[n], range(nblocks))
+            ps[n][:, half:] = jnp.dot(wide[n][...], x_ref[:, :tap_count], preferred_element_type=jnp.float32)
+            for raw_ref in inputs[n]:
+                for low in range(0, rows, LANES):
+                    squares = jnp.square(raw_ref[:, low : low + LANES].astype(jnp.float32))
+                    norms = norms + squares.reshape(-1, members, LANES).sum(axis=0)
+        norm_ref[...] = norms
+        lines = place_lines(shifted_sum(p_ref, members, 0, local_taps), route, local_taps, tap_count, width)
+        total = old_sum[...] + lines
+        main_ref[...] = total[:, tap_count:]
+        total = total[:, :tap_count]
+        for n in range(count):
+            lines = shifted_sum(ps[n], members, 0, local_taps)
+            total = total + place_lines(lines, routes[n], local_taps, tap_count, 2 * tap_count)[:, :tap_count]
+        pre_ref[:members, :] = total
+        pre_ref[members:, :] = before_ref[...]
+
+    operands = [masks, traces, sums, norm, products, before] + [part for shard in shards for part in shard]
+    wide_shape = pltpu.VMEM((flat, channels), jnp.bfloat16)
+    shapes = (
+        pltpu.VMEM((2 * members, tap_count), jnp.float32),
+        pltpu.VMEM((members, lags), jnp.float32),
+        pltpu.VMEM((members, LANES), jnp.float32),
+    ) + (wide_shape,) * count
+    return pl.pallas_call(
+        kernel,
+        out_shape=shapes,
+        in_specs=[VMEM] * len(operands),
+        out_specs=(VMEM,) * len(shapes),
+        scratch_shapes=[pltpu.VMEM((flat, half + tap_count), jnp.float32)] * count,
+        compiler_params=PARAMS,
+        name="edge",
+    )(*[resident(value) for value in operands])
+
+
+def last(traces, wides, routes, main, local_taps, tap_count):
+    flat, _ = wides[0].shape
+    members, lags = main.shape
+    half = tap_count // 2
+    count = len(wides)
+
+    def kernel(x_ref, old_main, *refs):
+        wide, main_ref, ps = refs[:count], refs[count], refs[count + 1 :]
+        total = old_main[...]
+        for n in range(count):
+            ps[n][:, :half] = jnp.zeros((flat, half), jnp.float32)
+        for n in range(count):
+            for start, size in column_pieces(lags):
+                ps[n][:, half + start : half + start + size] = jnp.dot(
+                    wide[n][...], x_ref[:, start : start + size], preferred_element_type=jnp.float32
+                )
+        for n in range(count):
+            lines = shifted_sum(ps[n], members, 0, local_taps)
+            total = total + place_lines(lines, routes[n], local_taps, tap_count, lags + tap_count)[:, tap_count:]
+        main_ref[...] = total
+
+    operands = [traces, main, *wides]
+    return pl.pallas_call(
+        kernel,
+        out_shape=pltpu.VMEM((members, lags), jnp.float32),
+        in_specs=[VMEM] * len(operands),
+        out_specs=VMEM,
+        scratch_shapes=[pltpu.VMEM((flat, half + lags), jnp.float32)] * count,
+        compiler_params=PARAMS,
+        name="last",
     )(*[resident(value) for value in operands])
 
 
@@ -354,9 +436,8 @@
 
     state = [None]
 
-    def take(shards, routes, final=None):
-        state[0] = absorb(masks, samples, shards, routes, state[0], final, local_taps, tap_count)
-        return state[0]
+    def take(shards, routes):
+        state[0] = absorb(masks, samples, shards, routes, state[0], local_taps, tap_count)
 
     far = send(own, lambda s, i: (s, i ^ far_route[s]))
     own_x = over_x(own)
@@ -385,8 +466,10 @@
     core_far_xy_0 = over_core(far_xy_0)
     core_far_xy_1 = over_core(far_xy_1)
     take([core_far_x, core_far_y], [pair(far_x_route)[1], pair(far_y_route)[1]])
-    main, norm, pre = take([[far_xy_0, far_xy_1], [core_far_xy_0, core_far_xy_1]], pair(far_xy_route), before)
+    ends = [[far_xy_0, far_xy_1], [core_far_xy_0, core_far_xy_1]]
+    pre, main, norm, *wides = edge(masks, samples, ends, pair(far_xy_route), state[0], before, local_taps, tap_count)
     after = send(pre, lambda s, i: (s, i - 1) if i > 0 else None)
+    main = last(samples, wides, pair(far_xy_route), main, local_taps, tap_count)
     return finish(main, norm, energy, after, math.sqrt(tap_count * row_count))
 
 

time: 55.4 us -> 52.9 us (0.955)
  waiting for transfers between devices: 20.2 us -> 18.1 us
  Pallas kernels: 17.8 us -> 17.1 us
    pallas_call x8 -> x7, Pallas kernels: 14.1 us -> 10.5 us  [absorb(): pl.pallas_call(kernel, out_shape=shapes, in_specs=[VMEM] * len(operands),...]
    pallas_call x0 -> x2, Pallas kernels: none -> 3 us  [the longest x1 1.62 us: last(): pl.pallas_call(kernel, out_shape=pltpu.VMEM((members, lags), jnp.float32)...]
    ppermute x18, waiting for transfers between devices: 20.2 us -> 18.1 us  [send(): return lax.ppermute(value, both, route)]
where the time goes in v1:
time: 52.9 us; the launch traced here: 52.7 us
  waiting for transfers between devices  18.1 us (34%)
  starting transfers between devices  17.3 us (33%)
  Pallas kernels  17.1 us (32%)
    ppermute x18, waiting for transfers between devices, send(): return lax.ppermute(value, both, route)  18.1 us
    ppermute x18, starting transfers between devices, send(): return lax.ppermute(value, both, route)  17.3 us
    pallas_call x7, Pallas kernels, absorb(): pl.pallas_call(kernel, out_shape=shapes, in_specs=[VMEM] * len(operands),...  10.5 us
    pallas_call x1, Pallas kernels, prepare(): pl.pallas_call(kernel, out_shape=(pltpu.VMEM((members, tap_count), jnp.fl...  2.92 us
    pallas_call x1, Pallas kernels, last(): pl.pallas_call(kernel, out_shape=pltpu.VMEM((members, lags), jnp.float32)...  1.62 us
    pallas_call x1, Pallas kernels, edge(): pl.pallas_call(kernel, out_shape=shapes, in_specs=[VMEM] * len(operands),...  1.38 us
  transfers between devices with their start and end apart: 18, of which 6 were waited for; matrix products, arithmetic and copies ran while one was open for 0% of the time, Pallas kernels for 28%

profile of v1, /device:TPU:11, one launch (start us, length us, event | category | flops | bytes accessed | tf_op | source)
XLA Modules:
  0.0 52.7 jit_solution(18357799977393742503)
XLA Ops:
  0.0 0.3 collective-permute-start.5
  0.3 2.3 %collective-permute-start = (bf16[256,512]{1,0:T(8,128)(2,1)}, bf16[256,512]{1,0:T(8,128)(2,1)S(1)}, u32[]{:S(2)}, u32[]{:S(2)}) collective-permute-start(bf16[256,512]{1,0:T(8,128)(2,1)} %bitcast.3), channel_id=1, source_target_pairs={{0,8},{1,9},{2,10},{3,11},{4,12},{5,13},{6,14},{7,15},{8,0},{9,1},... | collective-permute-start | bytes 786440 | tf_op jit(solution)/shard_map/ppermute | solution.py:415
  2.6 1.2 %collective-permute-start.12 = (bf16[256,512]{1,0:T(8,128)(2,1)}, bf16[256,512]{1,0:T(8,128)(2,1)S(1)}, u32[]{:S(2)}, u32[]{:S(2)}) collective-permute-start(bf16[256,512]{1,0:T(8,128)(2,1)} %bitcast.4), channel_id=1, source_target_pairs={{0,1},{1,0},{2,3},{3,2},{4,5},{5,4},{6,7},{7,6},{8,9},{9,8},{10,11... | collective-permute-start | bytes 786440 | tf_op jit(solution)/shard_map/ppermute | solution.py:415
  3.8 0.2 collective-permute-start.8
  4.0 3.4 %collective-permute-done.5.refs_0_ = bf16[256,512]{1,0:T(8,128)(2,1)S(1)} collective-permute-done((bf16[256,512]{1,0:T(8,128)(2,1)}, bf16[256,512]{1,0:T(8,128)(2,1)S(1)}, u32[]{:S(2)}, u32[]{:S(2)}) %collective-permute-start.5) | collective-permute-done | bytes 262176 | tf_op jit(solution)/shard_map/ppermute | solution.py:415
  7.4 0.2 collective-permute-start.6
  7.6 6.9 %collective-permute-done.refs_1_ = bf16[256,512]{1,0:T(8,128)(2,1)S(1)} collective-permute-done((bf16[256,512]{1,0:T(8,128)(2,1)}, bf16[256,512]{1,0:T(8,128)(2,1)S(1)}, u32[]{:S(2)}, u32[]{:S(2)}) %collective-permute-start) | collective-permute-done | bytes 262176 | tf_op jit(solution)/shard_map/ppermute | solution.py:415
  14.5 0.2 collective-permute-start.3
  14.7 1.2 %collective-permute-start.1 = (bf16[256,512]{1,0:T(8,128)(2,1)S(1)}, bf16[256,512]{1,0:T(8,128)(2,1)S(1)}, u32[]{:S(2)}, u32[]{:S(2)}) collective-permute-start(bf16[256,512]{1,0:T(8,128)(2,1)S(1)} %collective-permute-done.refs_1_), channel_id=1, source_target_pairs={{0,2},{1,3},{2,0},{3,1},{4,6},{5,7},{6,4},{7,5},{8,10},{9,11},{10,... | collective-permute-start | bytes 786440 | tf_op jit(solution)/shard_map/ppermute | solution.py:415
  15.9 0.0 collective-permute-done.12.refs_1_
  15.9 1.9 %collective-permute-start.11 = (bf16[256,512]{1,0:T(8,128)(2,1)S(1)}, bf16[256,512]{1,0:T(8,128)(2,1)S(1)}, u32[]{:S(2)}, u32[]{:S(2)}) collective-permute-start(bf16[256,512]{1,0:T(8,128)(2,1)S(1)} %collective-permute-done.5.refs_0_), channel_id=1, source_target_pairs={{0,1},{1,0},{2,3},{3,2},{4,5},{5,4},{6,7},{7,6},{8,9},{9,8},{10,11... | collective-permute-start | bytes 786440 | tf_op jit(solution)/shard_map/ppermute | solution.py:415
  17.8 0.0 collective-permute-done.8.refs_0_
  17.8 0.1 collective-permute-start.10
  17.9 2.0 %collective-permute-done.6.refs_0_ = bf16[256,512]{1,0:T(8,128)(2,1)S(1)} collective-permute-done((bf16[256,512]{1,0:T(8,128)(2,1)S(1)}, bf16[256,512]{1,0:T(8,128)(2,1)S(1)}, u32[]{:S(2)}, u32[]{:S(2)}) %collective-permute-start.6) | collective-permute-done | bytes 262176 | tf_op jit(solution)/shard_map/ppermute | solution.py:415
  19.9 1.6 %collective-permute-start.9 = (bf16[256,512]{1,0:T(8,128)(2,1)S(1)}, bf16[256,512]{1,0:T(8,128)(2,1)S(1)}, u32[]{:S(2)}, u32[]{:S(2)}) collective-permute-start(bf16[256,512]{1,0:T(8,128)(2,1)S(1)} %collective-permute-done.8.refs_0_), channel_id=1, source_target_pairs={{0,1},{1,0},{2,3},{3,2},{4,5},{5,4},{6,7},{7,6},{8,9},{9,8},{10,11... | collective-permute-start | bytes 786440 | tf_op jit(solution)/shard_map/ppermute | solution.py:415
  21.5 0.3 collective-permute-done.3.refs_1_
  21.8 1.3 %collective-permute-start.7 = (bf16[256,512]{1,0:T(8,128)(2,1)S(1)}, bf16[256,512]{1,0:T(8,128)(2,1)S(1)}, u32[]{:S(2)}, u32[]{:S(2)}) collective-permute-start(bf16[256,512]{1,0:T(8,128)(2,1)S(1)} %collective-permute-done.6.refs_0_), channel_id=1, source_target_pairs={{0,1},{1,0},{2,3},{3,2},{4,5},{5,4},{6,7},{7,6},{8,9},{9,8},{10,11... | collective-permute-start | bytes 786440 | tf_op jit(solution)/shard_map/ppermute | solution.py:415
  23.2 0.0 collective-permute-done.1.refs_0_
  23.2 0.2 collective-permute-start.2
  23.4 0.0 collective-permute-done.11.refs_1_
  23.4 0.4 collective-permute-start.4
  23.8 0.0 collective-permute-done.10.refs_1_
  23.8 1.3 %collective-permute-start.13 = (bf16[128,512]{1,0:T(8,128)(2,1)S(1)}, bf16[128,512]{1,0:T(8,128)(2,1)S(1)}, u32[]{:S(2)}, u32[]{:S(2)}) collective-permute-start(bf16[128,512]{1,0:T(8,128)(2,1)S(1)} %slice.8), channel_id=1, source_target_pairs={{0,2},{1,3},{2,0},{3,1},{4,6},{5,7},{6,4},{7,5},{8,10},{9,11},{10,... | collective-permute-start | bytes 393224 | tf_op jit(solution)/shard_map/ppermute | solution.py:415
  25.1 0.0 collective-permute-done.9.refs_0_
  25.1 0.9 %collective-permute-start.14 = (bf16[128,512]{1,0:T(8,128)(2,1)S(1)}, bf16[128,512]{1,0:T(8,128)(2,1)S(1)}, u32[]{:S(2)}, u32[]{:S(2)}) collective-permute-start(bf16[128,512]{1,0:T(8,128)(2,1)S(1)} %slice.9), channel_id=1, source_target_pairs={{0,16},{1,17},{2,18},{3,19},{4,20},{5,21},{6,22},{7,23},{8,24},{9,... | collective-permute-start | bytes 393224 | tf_op jit(solution)/shard_map/ppermute | solution.py:415
  26.0 2.8 %collective-permute-done.13.refs_0_ = bf16[128,512]{1,0:T(8,128)(2,1)S(1)} collective-permute-done((bf16[128,512]{1,0:T(8,128)(2,1)S(1)}, bf16[128,512]{1,0:T(8,128)(2,1)S(1)}, u32[]{:S(2)}, u32[]{:S(2)}) %collective-permute-start.13) | collective-permute-done | bytes 131104 | tf_op jit(solution)/shard_map/ppermute | solution.py:415
  28.8 1.0 %collective-permute-start.15 = (bf16[128,512]{1,0:T(8,128)(2,1)S(1)}, bf16[128,512]{1,0:T(8,128)(2,1)S(1)}, u32[]{:S(2)}, u32[]{:S(2)}) collective-permute-start(bf16[128,512]{1,0:T(8,128)(2,1)S(1)} %collective-permute-done.13.refs_0_), channel_id=1, source_target_pairs={{0,1},{1,0},{2,3},{3,2},{4,5},{5,4},{6,7},{7,6},{8,9},{9,8},{10,11... | collective-permute-start | bytes 393224 | tf_op jit(solution)/shard_map/ppermute | solution.py:415
  29.8 0.0 collective-permute-done.14.refs_1_
  29.8 1.2 %collective-permute-start.16 = (bf16[128,512]{1,0:T(8,128)(2,1)S(1)}, bf16[128,512]{1,0:T(8,128)(2,1)S(1)}, u32[]{:S(2)}, u32[]{:S(2)}) collective-permute-start(bf16[128,512]{1,0:T(8,128)(2,1)S(1)} %collective-permute-done.14.refs_1_), channel_id=1, source_target_pairs={{0,1},{1,0},{2,3},{3,2},{4,5},{5,4},{6,7},{7,6},{8,9},{9,8},{10,11... | collective-permute-start | bytes 393224 | tf_op jit(solution)/shard_map/ppermute | solution.py:415
  31.0 2.9 %prepare.1 = (f32[16,256]{1,0:T(8,128)S(1)}, f32[16,1024]{1,0:T(8,128)S(1)}, bf16[4,8,16,128]{3,2,1,0:T(8,128)(2,1)S(1)}, bf16[1024,1024]{1,0:T(8,128)(2,1)S(1)}, bf16[256,512]{1,0:T(8,128)(2,1)S(1)}) custom-call(s32[4,16]{1,0:T(4,128)} %bitcast.7, bf16[1024,1024]{1,0:T(8,128)(2,1)} %x_hbm.1, bf16[256,512]{1,0:T(8,128)(2,1)} %bitcast.6), custom_call_target="tpu_custom_call" | custom-call | tf_op jit(solution)/shard_map/prepare/pallas_call | solution.py:131
  33.9 1.4 %shard_map.37 = (f32[16,1280]{1,0:T(8,128)S(1)}, f32[16,128]{1,0:T(8,128)S(1)}, f32[256,1152]{1,0:T(8,128)S(1)}) custom-call(bf16[4,8,16,128]{3,2,1,0:T(8,128)(2,1)S(1)} %get-tuple-element.37.mask_ref, bf16[1024,1024]{1,0:T(8,128)(2,1)S(1)} %get-tuple-element.36.x_ref, bf16[256,512]{1,0:T(8,128)(2,1)S(1)} %get-tuple-element.38.refs_0_, ...), custom_call_target="tpu_custom_call" | custom-call | tf_op jit(solution)/shard_map/pallas_call | solution.py:270
  35.3 1.6 %shard_map.38 = (f32[16,1280]{1,0:T(8,128)S(1)}, f32[16,128]{1,0:T(8,128)S(1)}, f32[256,1152]{1,0:T(8,128)S(1)}) custom-call(bf16[4,8,16,128]{3,2,1,0:T(8,128)(2,1)S(1)} %get-tuple-element.37.mask_ref, bf16[1024,1024]{1,0:T(8,128)(2,1)S(1)} %get-tuple-element.36.x_ref, bf16[256,512]{1,0:T(8,128)(2,1)S(1)} %collective-permute-done.5.refs_0_, ...), custom_call_target="tpu_custom_call" | custom-call | tf_op jit(solution)/shard_map/pallas_call | solution.py:270
  36.9 1.5 %shard_map.39 = (f32[16,1280]{1,0:T(8,128)S(1)}, f32[16,128]{1,0:T(8,128)S(1)}, f32[256,1152]{1,0:T(8,128)S(1)}) custom-call(bf16[4,8,16,128]{3,2,1,0:T(8,128)(2,1)S(1)} %get-tuple-element.37.mask_ref, bf16[1024,1024]{1,0:T(8,128)(2,1)S(1)} %get-tuple-element.36.x_ref, bf16[256,512]{1,0:T(8,128)(2,1)S(1)} %collective-permute-done.8.refs_0_, ...), custom_call_target="tpu_custom_call" | custom-call | tf_op jit(solution)/shard_map/pallas_call | solution.py:270
  38.4 1.5 %shard_map.40 = (f32[16,1280]{1,0:T(8,128)S(1)}, f32[16,128]{1,0:T(8,128)S(1)}, f32[256,1152]{1,0:T(8,128)S(1)}) custom-call(bf16[4,8,16,128]{3,2,1,0:T(8,128)(2,1)S(1)} %get-tuple-element.37.mask_ref, bf16[1024,1024]{1,0:T(8,128)(2,1)S(1)} %get-tuple-element.36.x_ref, bf16[256,512]{1,0:T(8,128)(2,1)S(1)} %collective-permute-done.9.refs_0_, ...), custom_call_target="tpu_custom_call" | custom-call | tf_op jit(solution)/shard_map/pallas_call | solution.py:270
  40.0 0.8 %shard_map.41 = (f32[16,1280]{1,0:T(8,128)S(1)}, f32[16,128]{1,0:T(8,128)S(1)}, f32[256,1152]{1,0:T(8,128)S(1)}) custom-call(bf16[4,8,16,128]{3,2,1,0:T(8,128)(2,1)S(1)} %get-tuple-element.37.mask_ref, bf16[1024,1024]{1,0:T(8,128)(2,1)S(1)} %get-tuple-element.36.x_ref, bf16[256,512]{1,0:T(8,128)(2,1)S(1)} %collective-permute-done.6.refs_0_, ...), custom_call_target="tpu_custom_call" | custom-call | tf_op jit(solution)/shard_map/pallas_call | solution.py:270
  40.8 0.0 collective-permute-done.7.refs_2_
  40.8 2.1 %shard_map.42 = (f32[16,1280]{1,0:T(8,128)S(1)}, f32[16,128]{1,0:T(8,128)S(1)}, f32[256,1152]{1,0:T(8,128)S(1)}) custom-call(bf16[4,8,16,128]{3,2,1,0:T(8,128)(2,1)S(1)} %get-tuple-element.37.mask_ref, bf16[1024,1024]{1,0:T(8,128)(2,1)S(1)} %get-tuple-element.36.x_ref, bf16[256,512]{1,0:T(8,128)(2,1)S(1)} %collective-permute-done.1.refs_0_, ...), custom_call_target="tpu_custom_call" | custom-call | tf_op jit(solution)/shard_map/pallas_call | solution.py:270
  42.9 0.0 collective-permute-done.2.refs_0_
  42.9 0.0 collective-permute-done.4.refs_1_
  43.0 1.5 %shard_map.43 = (f32[16,1280]{1,0:T(8,128)S(1)}, f32[16,128]{1,0:T(8,128)S(1)}, f32[256,1152]{1,0:T(8,128)S(1)}) custom-call(bf16[4,8,16,128]{3,2,1,0:T(8,128)(2,1)S(1)} %get-tuple-element.37.mask_ref, bf16[1024,1024]{1,0:T(8,128)(2,1)S(1)} %get-tuple-element.36.x_ref, bf16[256,512]{1,0:T(8,128)(2,1)S(1)} %collective-permute-done.2.refs_0_, ...), custom_call_target="tpu_custom_call" | custom-call | tf_op jit(solution)/shard_map/pallas_call | solution.py:270
  44.5 0.0 collective-permute-done.15.refs_2_
  44.5 0.0 collective-permute-done.16.refs_3_
  44.5 1.4 %edge.1 = (f32[32,256]{1,0:T(8,128)S(1)}, f32[16,1024]{1,0:T(8,128)S(1)}, f32[16,128]{1,0:T(8,128)S(1)}, bf16[256,1024]{1,0:T(8,128)(2,1)S(1)}, bf16[256,1024]{1,0:T(8,128)(2,1)S(1)}) custom-call(bf16[4,8,16,128]{3,2,1,0:T(8,128)(2,1)S(1)} %get-tuple-element.37.mask_ref, bf16[1024,1024]{1,0:T(8,128)(2,1)S(1)} %get-tuple-element.36.x_ref, ...), custom_call_target="tpu_custom_call" | custom-call | tf_op jit(solution)/shard_map/edge/pallas_call | solution.py:332
  45.9 1.9 %collective-permute-start.17 = (f32[32,256]{1,0:T(8,128)S(1)}, f32[32,256]{1,0:T(8,128)S(1)}, u32[]{:S(2)}, u32[]{:S(2)}) collective-permute-start(f32[32,256]{1,0:T(8,128)S(1)} %get-tuple-element.66), channel_id=1, source_target_pairs={{1,0},{2,1},{3,2},{4,3},{5,4},{6,5},{7,6},{8,7},{9,8},{10,9},{11,1... | collective-permute-start | bytes 98312 | tf_op jit(solution)/shard_map/ppermute | solution.py:415
  47.8 1.6 %last.1.main_ref = f32[16,1024]{1,0:T(8,128)S(1)} custom-call(bf16[1024,1024]{1,0:T(8,128)(2,1)S(1)} %get-tuple-element.36.x_ref, f32[16,1024]{1,0:T(8,128)S(1)} %get-tuple-element.61.old_main, bf16[256,1024]{1,0:T(8,128)(2,1)S(1)} %get-tuple-element.62.refs_0_, bf16[256,1024]{1,0:T(8,128)(2,1)S(1)} %get-tuple-element.63.refs_1_), custom_call_target="tpu_custom_call" | custom-call | tf_op jit(solution)/shard_map/last/pallas_call | solution.py:365
  49.4 2.6 %collective-permute-done.17.after_ref = f32[32,256]{1,0:T(8,128)S(1)} collective-permute-done((f32[32,256]{1,0:T(8,128)S(1)}, f32[32,256]{1,0:T(8,128)S(1)}, u32[]{:S(2)}, u32[]{:S(2)}) %collective-permute-start.17) | collective-permute-done | bytes 32800 | tf_op jit(solution)/shard_map/ppermute | solution.py:415
  52.0 0.7 %finish.1 = f32[16,1024]{1,0:T(8,128)} custom-call(f32[16,1024]{1,0:T(8,128)S(1)} %last.1.main_ref, f32[16,128]{1,0:T(8,128)S(1)} %get-tuple-element.64.norm_ref, f32[16,1024]{1,0:T(8,128)S(1)} %get-tuple-element.65.energy_ref, f32[32,256]{1,0:T(8,128)S(1)} %collective-permute-done.17.after_ref), custom_call_target="tpu_custom_call" | custom-call | tf_op jit(solution)/shard_map/finish/pallas_call | solution.py:388
  (2 shorter events, 0.0 us)
Async XLA Ops:
  0.0 7.4 %collective-permute-start.5 = (bf16[256,512]{1,0:T(8,128)(2,1)}, bf16[256,512]{1,0:T(8,128)(2,1)S(1)}, u32[]{:S(2)}, u32[]{:S(2)}) collective-permute-start(bf16[256,512]{1,0:T(8,128)(2,1)} %bitcast.2), channel_id=1, source_target_pairs={{0,2},{1,3},{2,0},{3,1},{4,6},{5,7},{6,4},{7,5},{8,10},{9,11},{10,... | collective-permute-start | bytes 786440 | tf_op jit(solution)/shard_map/ppermute | solution.py:415
  0.3 14.2 %collective-permute-start = (bf16[256,512]{1,0:T(8,128)(2,1)}, bf16[256,512]{1,0:T(8,128)(2,1)S(1)}, u32[]{:S(2)}, u32[]{:S(2)}) collective-permute-start(bf16[256,512]{1,0:T(8,128)(2,1)} %bitcast.3), channel_id=1, source_target_pairs={{0,8},{1,9},{2,10},{3,11},{4,12},{5,13},{6,14},{7,15},{8,0},{9,1},... | collective-permute-start | bytes 786440 | tf_op jit(solution)/shard_map/ppermute | solution.py:415
  2.6 13.3 %collective-permute-start.12 = (bf16[256,512]{1,0:T(8,128)(2,1)}, bf16[256,512]{1,0:T(8,128)(2,1)S(1)}, u32[]{:S(2)}, u32[]{:S(2)}) collective-permute-start(bf16[256,512]{1,0:T(8,128)(2,1)} %bitcast.4), channel_id=1, source_target_pairs={{0,1},{1,0},{2,3},{3,2},{4,5},{5,4},{6,7},{7,6},{8,9},{9,8},{10,11... | collective-permute-start | bytes 786440 | tf_op jit(solution)/shard_map/ppermute | solution.py:415
  3.8 14.0 %collective-permute-start.8 = (bf16[256,512]{1,0:T(8,128)(2,1)}, bf16[256,512]{1,0:T(8,128)(2,1)S(1)}, u32[]{:S(2)}, u32[]{:S(2)}) collective-permute-start(bf16[256,512]{1,0:T(8,128)(2,1)} %bitcast.5), channel_id=1, source_target_pairs={{0,4},{1,5},{2,6},{3,7},{4,0},{5,1},{6,2},{7,3},{8,12},{9,13},{10,... | collective-permute-start | bytes 786440 | tf_op jit(solution)/shard_map/ppermute | solution.py:415
  7.4 12.5 %collective-permute-start.6 = (bf16[256,512]{1,0:T(8,128)(2,1)S(1)}, bf16[256,512]{1,0:T(8,128)(2,1)S(1)}, u32[]{:S(2)}, u32[]{:S(2)}) collective-permute-start(bf16[256,512]{1,0:T(8,128)(2,1)S(1)} %collective-permute-done.5.refs_0_), channel_id=1, source_target_pairs={{0,4},{1,5},{2,6},{3,7},{4,0},{5,1},{6,2},{7,3},{8,12},{9,13},{10,... | collective-permute-start | bytes 786440 | tf_op jit(solution)/shard_map/ppermute | solution.py:415
  14.5 7.4 %collective-permute-start.3 = (bf16[256,512]{1,0:T(8,128)(2,1)S(1)}, bf16[256,512]{1,0:T(8,128)(2,1)S(1)}, u32[]{:S(2)}, u32[]{:S(2)}) collective-permute-start(bf16[256,512]{1,0:T(8,128)(2,1)S(1)} %collective-permute-done.refs_1_), channel_id=1, source_target_pairs={{0,16},{1,17},{2,18},{3,19},{4,20},{5,21},{6,22},{7,23},{8,24},{9,... | collective-permute-start | bytes 786440 | tf_op jit(solution)/shard_map/ppermute | solution.py:415
  14.7 8.5 %collective-permute-start.1 = (bf16[256,512]{1,0:T(8,128)(2,1)S(1)}, bf16[256,512]{1,0:T(8,128)(2,1)S(1)}, u32[]{:S(2)}, u32[]{:S(2)}) collective-permute-start(bf16[256,512]{1,0:T(8,128)(2,1)S(1)} %collective-permute-done.refs_1_), channel_id=1, source_target_pairs={{0,2},{1,3},{2,0},{3,1},{4,6},{5,7},{6,4},{7,5},{8,10},{9,11},{10,... | collective-permute-start | bytes 786440 | tf_op jit(solution)/shard_map/ppermute | solution.py:415
  15.9 7.5 %collective-permute-start.11 = (bf16[256,512]{1,0:T(8,128)(2,1)S(1)}, bf16[256,512]{1,0:T(8,128)(2,1)S(1)}, u32[]{:S(2)}, u32[]{:S(2)}) collective-permute-start(bf16[256,512]{1,0:T(8,128)(2,1)S(1)} %collective-permute-done.5.refs_0_), channel_id=1, source_target_pairs={{0,1},{1,0},{2,3},{3,2},{4,5},{5,4},{6,7},{7,6},{8,9},{9,8},{10,11... | collective-permute-start | bytes 786440 | tf_op jit(solution)/shard_map/ppermute | solution.py:415
  17.8 6.0 %collective-permute-start.10 = (bf16[256,512]{1,0:T(8,128)(2,1)S(1)}, bf16[256,512]{1,0:T(8,128)(2,1)S(1)}, u32[]{:S(2)}, u32[]{:S(2)}) collective-permute-start(bf16[256,512]{1,0:T(8,128)(2,1)S(1)} %collective-permute-done.refs_1_), channel_id=1, source_target_pairs={{0,1},{1,0},{2,3},{3,2},{4,5},{5,4},{6,7},{7,6},{8,9},{9,8},{10,11... | collective-permute-start | bytes 786440 | tf_op jit(solution)/shard_map/ppermute | solution.py:415
  19.9 5.2 %collective-permute-start.9 = (bf16[256,512]{1,0:T(8,128)(2,1)S(1)}, bf16[256,512]{1,0:T(8,128)(2,1)S(1)}, u32[]{:S(2)}, u32[]{:S(2)}) collective-permute-start(bf16[256,512]{1,0:T(8,128)(2,1)S(1)} %collective-permute-done.8.refs_0_), channel_id=1, source_target_pairs={{0,1},{1,0},{2,3},{3,2},{4,5},{5,4},{6,7},{7,6},{8,9},{9,8},{10,11... | collective-permute-start | bytes 786440 | tf_op jit(solution)/shard_map/ppermute | solution.py:415
  21.8 18.9 %collective-permute-start.7 = (bf16[256,512]{1,0:T(8,128)(2,1)S(1)}, bf16[256,512]{1,0:T(8,128)(2,1)S(1)}, u32[]{:S(2)}, u32[]{:S(2)}) collective-permute-start(bf16[256,512]{1,0:T(8,128)(2,1)S(1)} %collective-permute-done.6.refs_0_), channel_id=1, source_target_pairs={{0,1},{1,0},{2,3},{3,2},{4,5},{5,4},{6,7},{7,6},{8,9},{9,8},{10,11... | collective-permute-start | bytes 786440 | tf_op jit(solution)/shard_map/ppermute | solution.py:415
  23.2 19.7 %collective-permute-start.2 = (bf16[256,512]{1,0:T(8,128)(2,1)S(1)}, bf16[256,512]{1,0:T(8,128)(2,1)S(1)}, u32[]{:S(2)}, u32[]{:S(2)}) collective-permute-start(bf16[256,512]{1,0:T(8,128)(2,1)S(1)} %collective-permute-done.1.refs_0_), channel_id=1, source_target_pairs={{0,1},{1,0},{2,3},{3,2},{4,5},{5,4},{6,7},{7,6},{8,9},{9,8},{10,11... | collective-permute-start | bytes 786440 | tf_op jit(solution)/shard_map/ppermute | solution.py:415
  23.4 19.6 %collective-permute-start.4 = (bf16[256,512]{1,0:T(8,128)(2,1)S(1)}, bf16[256,512]{1,0:T(8,128)(2,1)S(1)}, u32[]{:S(2)}, u32[]{:S(2)}) collective-permute-start(bf16[256,512]{1,0:T(8,128)(2,1)S(1)} %collective-permute-done.3.refs_1_), channel_id=1, source_target_pairs={{0,1},{1,0},{2,3},{3,2},{4,5},{5,4},{6,7},{7,6},{8,9},{9,8},{10,11... | collective-permute-start | bytes 786440 | tf_op jit(solution)/shard_map/ppermute | solution.py:415
  23.8 5.0 %collective-permute-start.13 = (bf16[128,512]{1,0:T(8,128)(2,1)S(1)}, bf16[128,512]{1,0:T(8,128)(2,1)S(1)}, u32[]{:S(2)}, u32[]{:S(2)}) collective-permute-start(bf16[128,512]{1,0:T(8,128)(2,1)S(1)} %slice.8), channel_id=1, source_target_pairs={{0,2},{1,3},{2,0},{3,1},{4,6},{5,7},{6,4},{7,5},{8,10},{9,11},{10,... | collective-permute-start | bytes 393224 | tf_op jit(solution)/shard_map/ppermute | solution.py:415
  25.1 4.7 %collective-permute-start.14 = (bf16[128,512]{1,0:T(8,128)(2,1)S(1)}, bf16[128,512]{1,0:T(8,128)(2,1)S(1)}, u32[]{:S(2)}, u32[]{:S(2)}) collective-permute-start(bf16[128,512]{1,0:T(8,128)(2,1)S(1)} %slice.9), channel_id=1, source_target_pairs={{0,16},{1,17},{2,18},{3,19},{4,20},{5,21},{6,22},{7,23},{8,24},{9,... | collective-permute-start | bytes 393224 | tf_op jit(solution)/shard_map/ppermute | solution.py:415
  28.8 15.7 %collective-permute-start.15 = (bf16[128,512]{1,0:T(8,128)(2,1)S(1)}, bf16[128,512]{1,0:T(8,128)(2,1)S(1)}, u32[]{:S(2)}, u32[]{:S(2)}) collective-permute-start(bf16[128,512]{1,0:T(8,128)(2,1)S(1)} %collective-permute-done.13.refs_0_), channel_id=1, source_target_pairs={{0,1},{1,0},{2,3},{3,2},{4,5},{5,4},{6,7},{7,6},{8,9},{9,8},{10,11... | collective-permute-start | bytes 393224 | tf_op jit(solution)/shard_map/ppermute | solution.py:415
  29.8 14.7 %collective-permute-start.16 = (bf16[128,512]{1,0:T(8,128)(2,1)S(1)}, bf16[128,512]{1,0:T(8,128)(2,1)S(1)}, u32[]{:S(2)}, u32[]{:S(2)}) collective-permute-start(bf16[128,512]{1,0:T(8,128)(2,1)S(1)} %collective-permute-done.14.refs_1_), channel_id=1, source_target_pairs={{0,1},{1,0},{2,3},{3,2},{4,5},{5,4},{6,7},{7,6},{8,9},{9,8},{10,11... | collective-permute-start | bytes 393224 | tf_op jit(solution)/shard_map/ppermute | solution.py:415
  45.9 6.1 %collective-permute-start.17 = (f32[32,256]{1,0:T(8,128)S(1)}, f32[32,256]{1,0:T(8,128)S(1)}, u32[]{:S(2)}, u32[]{:S(2)}) collective-permute-start(f32[32,256]{1,0:T(8,128)S(1)} %get-tuple-element.66), channel_id=1, source_target_pairs={{1,0},{2,1},{3,2},{4,3},{5,4},{6,5},{7,6},{8,7},{9,8},{10,9},{11,1... | collective-permute-start | bytes 98312 | tf_op jit(solution)/shard_map/ppermute | solution.py:415

commit v2 on v1

--- a/solution.py
+++ b/solution.py
@@ -285,50 +285,41 @@
 
 
 def edge(masks, traces, shards, routes, carried, before, local_taps, tap_count):
-    sums, norm, products, route = carried
-    flat, rows = sum(part.shape[0] for part in shards[0]), shards[0][0].shape[1]
-    members, width = sums.shape
-    channels, lags = traces.shape
+    sums, _, products, route = carried
+    flat = sum(part.shape[0] for part in shards[0])
+    members = sums.shape[0]
+    channels = traces.shape[0]
     half = tap_count // 2
     count = len(shards)
     nblocks = masks.shape[1]
     lengths = [len(shard) for shard in shards]
 
-    def kernel(mask_ref, x_ref, old_sum, old_norm, p_ref, before_ref, *refs):
+    def kernel(mask_ref, x_ref, old_sum, p_ref, before_ref, *refs):
         inputs = []
         for length in lengths:
             inputs.append(refs[:length])
             refs = refs[length:]
-        pre_ref, main_ref, norm_ref = refs[:3]
-        wide, ps = refs[3 : 3 + count], refs[3 + count :]
+        pre_ref, wide, ps = refs[0], refs[1 : 1 + count], refs[1 + count :]
+        total = old_sum[:, :tap_count]
+
+        def add(total, p, origin):
+            lines = shifted_sum(p.at[:, : half + tap_count], members, 0, local_taps)
+            return total + place_lines(lines, origin, local_taps, tap_count, 2 * tap_count)[:, :tap_count]
+
         for p in ps:
             p[:, :half] = jnp.zeros((flat, half), jnp.float32)
-        norms = old_norm[...]
         for n in range(count):
             spread(mask_ref, inputs[n], wide[n], range(nblocks))
             ps[n][:, half:] = jnp.dot(wide[n][...], x_ref[:, :tap_count], preferred_element_type=jnp.float32)
-            for raw_ref in inputs[n]:
-                for low in range(0, rows, LANES):
-                    squares = jnp.square(raw_ref[:, low : low + LANES].astype(jnp.float32))
-                    norms = norms + squares.reshape(-1, members, LANES).sum(axis=0)
-        norm_ref[...] = norms
-        lines = place_lines(shifted_sum(p_ref, members, 0, local_taps), route, local_taps, tap_count, width)
-        total = old_sum[...] + lines
-        main_ref[...] = total[:, tap_count:]
-        total = total[:, :tap_count]
+            if n == 0:
+                total = add(total, p_ref, route)
         for n in range(count):
-            lines = shifted_sum(ps[n], members, 0, local_taps)
-            total = total + place_lines(lines, routes[n], local_taps, tap_count, 2 * tap_count)[:, :tap_count]
+            total = add(total, ps[n], routes[n])
         pre_ref[:members, :] = total
         pre_ref[members:, :] = before_ref[...]
 
-    operands = [masks, traces, sums, norm, products, before] + [part for shard in shards for part in shard]
-    wide_shape = pltpu.VMEM((flat, channels), jnp.bfloat16)
-    shapes = (
-        pltpu.VMEM((2 * members, tap_count), jnp.float32),
-        pltpu.VMEM((members, lags), jnp.float32),
-        pltpu.VMEM((members, LANES), jnp.float32),
-    ) + (wide_shape,) * count
+    operands = [masks, traces, sums, products, before] + [part for shard in shards for part in shard]
+    shapes = (pltpu.VMEM((2 * members, tap_count), jnp.float32),) + (pltpu.VMEM((flat, channels), jnp.bfloat16),) * count
     return pl.pallas_call(
         kernel,
         out_shape=shapes,
@@ -340,33 +331,51 @@
     )(*[resident(value) for value in operands])
 
 
-def last(traces, wides, routes, main, local_taps, tap_count):
+def last(traces, wides, shards, routes, carried, local_taps, tap_count):
+    sums, norm, products, route = carried
     flat, _ = wides[0].shape
-    members, lags = main.shape
+    members, width = sums.shape
+    lags = width - tap_count
     half = tap_count // 2
     count = len(wides)
-
-    def kernel(x_ref, old_main, *refs):
-        wide, main_ref, ps = refs[:count], refs[count], refs[count + 1 :]
-        total = old_main[...]
+    parts = [part for shard in shards for part in shard]
+    rows = parts[0].shape[1]
+
+    def kernel(x_ref, old_sum, old_norm, p_ref, *refs):
+        wide, refs = refs[:count], refs[count:]
+        inputs, (main_ref, norm_ref, *ps) = refs[: len(parts)], refs[len(parts) :]
         for n in range(count):
             ps[n][:, :half] = jnp.zeros((flat, half), jnp.float32)
+
+        def add(p, origin):
+            lines = shifted_sum(p, members, 0, local_taps)
+            main_ref[...] += place_lines(lines, origin, local_taps, tap_count, width)[:, tap_count:]
+
+        main_ref[...] = old_sum[:, tap_count:]
+        norms = old_norm[...]
         for n in range(count):
             for start, size in column_pieces(lags):
                 ps[n][:, half + start : half + start + size] = jnp.dot(
                     wide[n][...], x_ref[:, start : start + size], preferred_element_type=jnp.float32
                 )
-        for n in range(count):
-            lines = shifted_sum(ps[n], members, 0, local_taps)
-            total = total + place_lines(lines, routes[n], local_taps, tap_count, lags + tap_count)[:, tap_count:]
-        main_ref[...] = total
-
-    operands = [traces, main, *wides]
+                if n == 0 and start == 0:
+                    add(p_ref, route)
+            if n == 0:
+                for raw_ref in inputs:
+                    for low in range(0, rows, LANES):
+                        squares = jnp.square(raw_ref[:, low : low + LANES].astype(jnp.float32))
+                        norms = norms + squares.reshape(-1, members, LANES).sum(axis=0)
+            if n > 0:
+                add(ps[n - 1], routes[n - 1])
+        norm_ref[...] = norms
+        add(ps[count - 1], routes[count - 1])
+
+    operands = [traces, sums, norm, products, *wides, *parts]
     return pl.pallas_call(
         kernel,
-        out_shape=pltpu.VMEM((members, lags), jnp.float32),
+        out_shape=(pltpu.VMEM((members, lags), jnp.float32), pltpu.VMEM((members, LANES), jnp.float32)),
         in_specs=[VMEM] * len(operands),
-        out_specs=VMEM,
+        out_specs=(VMEM, VMEM),
         scratch_shapes=[pltpu.VMEM((flat, half + lags), jnp.float32)] * count,
         compiler_params=PARAMS,
         name="last",
@@ -427,7 +436,7 @@
         return send(value, lambda s, i: (s, i ^ 4))
 
     own = templates.reshape(local_taps * members, row_count)
-    part = own.shape[0] // 2
+    part = own.shape[0] * 3 // 8
     own_route, own_x_route, near_route, near_x_route = (0, 0), (2, 2), (4, 4), (6, 6)
     far_route, far_x_route, far_y_route, far_xy_route = (8, 12), (10, 14), (12, 8), (14, 10)
 
@@ -467,9 +476,11 @@
     core_far_xy_1 = over_core(far_xy_1)
     take([core_far_x, core_far_y], [pair(far_x_route)[1], pair(far_y_route)[1]])
     ends = [[far_xy_0, far_xy_1], [core_far_xy_0, core_far_xy_1]]
-    pre, main, norm, *wides = edge(masks, samples, ends, pair(far_xy_route), state[0], before, local_taps, tap_count)
+    pre, *wides = edge(
+        masks, samples, ends, pair(far_xy_route), state[0], before, local_taps, tap_count
+    )
     after = send(pre, lambda s, i: (s, i - 1) if i > 0 else None)
-    main = last(samples, wides, pair(far_xy_route), main, local_taps, tap_count)
+    main, norm = last(samples, wides, ends, pair(far_xy_route), state[0], local_taps, tap_count)
     return finish(main, norm, energy, after, math.sqrt(tap_count * row_count))
 
 

time: 52.9 us -> 53.9 us (1.019); the launches traced: 52.7 us -> 53.1 us
  waiting for transfers between devices: 18.1 us -> 21.1 us
  starting transfers between devices: 17.3 us -> 14.8 us
    ppermute x18, waiting for transfers between devices: 18.1 us -> 21.1 us  [send(): return lax.ppermute(value, both, route)]
    ppermute x18, starting transfers between devices: 17.3 us -> 14.8 us  [send(): return lax.ppermute(value, both, route)]
  transfers between devices with their start and end apart: 18 -> 18, of which waited for: 6 -> 5; matrix products, arithmetic and copies ran while one was open for 0% -> 0% of each run, Pallas kernels for 28% -> 29%
where the time goes in v2:
time: 53.9 us; the launch traced here: 53.1 us
  waiting for transfers between devices  21.1 us (39%)
  Pallas kernels  17.1 us (32%)
  starting transfers between devices  14.8 us (27%)
    ppermute x18, waiting for transfers between devices, send(): return lax.ppermute(value, both, route)  21.1 us
    ppermute x18, starting transfers between devices, send(): return lax.ppermute(value, both, route)  14.8 us
    pallas_call x7, Pallas kernels, absorb(): pl.pallas_call(kernel, out_shape=shapes, in_specs=[VMEM] * len(operands),...  10.5 us
    pallas_call x1, Pallas kernels, prepare(): pl.pallas_call(kernel, out_shape=(pltpu.VMEM((members, tap_count), jnp.fl...  2.92 us
    pallas_call x1, Pallas kernels, last(): pl.pallas_call(kernel, out_shape=(pltpu.VMEM((members, lags), jnp.float32...  1.95 us
  transfers between devices with their start and end apart: 18, of which 5 were waited for; matrix products, arithmetic and copies ran while one was open for 0% of the time, Pallas kernels for 29%

profile of v2, /device:TPU:11, one launch (start us, length us, event | category | flops | bytes accessed | tf_op | source)
XLA Modules:
  0.0 53.1 jit_solution(15034951377174727349)
XLA Ops:
  0.0 2.3 %collective-permute-start = (bf16[256,512]{1,0:T(8,128)(2,1)}, bf16[256,512]{1,0:T(8,128)(2,1)S(1)}, u32[]{:S(2)}, u32[]{:S(2)}) collective-permute-start(bf16[256,512]{1,0:T(8,128)(2,1)} %bitcast.2), channel_id=1, source_target_pairs={{0,8},{1,9},{2,10},{3,11},{4,12},{5,13},{6,14},{7,15},{8,0},{9,1},... | collective-permute-start | bytes 786440 | tf_op jit(solution)/shard_map/ppermute | solution.py:424
  2.3 0.3 collective-permute-start.5
  2.6 1.2 %collective-permute-start.12 = (bf16[256,512]{1,0:T(8,128)(2,1)}, bf16[256,512]{1,0:T(8,128)(2,1)S(1)}, u32[]{:S(2)}, u32[]{:S(2)}) collective-permute-start(bf16[256,512]{1,0:T(8,128)(2,1)} %bitcast.4), channel_id=1, source_target_pairs={{0,1},{1,0},{2,3},{3,2},{4,5},{5,4},{6,7},{7,6},{8,9},{9,8},{10,11... | collective-permute-start | bytes 786440 | tf_op jit(solution)/shard_map/ppermute | solution.py:424
  3.8 0.2 collective-permute-start.8
  4.0 10.2 %collective-permute-done.refs_1_ = bf16[256,512]{1,0:T(8,128)(2,1)S(1)} collective-permute-done((bf16[256,512]{1,0:T(8,128)(2,1)}, bf16[256,512]{1,0:T(8,128)(2,1)S(1)}, u32[]{:S(2)}, u32[]{:S(2)}) %collective-permute-start) | collective-permute-done | bytes 262176 | tf_op jit(solution)/shard_map/ppermute | solution.py:424
  14.2 0.3 collective-permute-start.1
  14.5 0.0 collective-permute-done.5.refs_0_
  14.5 0.8 %collective-permute-start.11 = (bf16[256,512]{1,0:T(8,128)(2,1)S(1)}, bf16[256,512]{1,0:T(8,128)(2,1)S(1)}, u32[]{:S(2)}, u32[]{:S(2)}) collective-permute-start(bf16[256,512]{1,0:T(8,128)(2,1)S(1)} %collective-permute-done.5.refs_0_), channel_id=1, source_target_pairs={{0,1},{1,0},{2,3},{3,2},{4,5},{5,4},{6,7},{7,6},{8,9},{9,8},{10,11... | collective-permute-start | bytes 786440 | tf_op jit(solution)/shard_map/ppermute | solution.py:424
  15.2 1.0 %collective-permute-start.6 = (bf16[256,512]{1,0:T(8,128)(2,1)S(1)}, bf16[256,512]{1,0:T(8,128)(2,1)S(1)}, u32[]{:S(2)}, u32[]{:S(2)}) collective-permute-start(bf16[256,512]{1,0:T(8,128)(2,1)S(1)} %collective-permute-done.5.refs_0_), channel_id=1, source_target_pairs={{0,4},{1,5},{2,6},{3,7},{4,0},{5,1},{6,2},{7,3},{8,12},{9,13},{10,... | collective-permute-start | bytes 786440 | tf_op jit(solution)/shard_map/ppermute | solution.py:424
  16.2 0.0 collective-permute-done.12.refs_1_
  16.2 0.3 collective-permute-start.10
  16.5 0.0 collective-permute-done.8.refs_0_
  16.5 0.0 collective-permute-start.3
  16.5 5.1 %collective-permute-done.1.refs_0_ = bf16[256,512]{1,0:T(8,128)(2,1)S(1)} collective-permute-done((bf16[256,512]{1,0:T(8,128)(2,1)S(1)}, bf16[256,512]{1,0:T(8,128)(2,1)S(1)}, u32[]{:S(2)}, u32[]{:S(2)}) %collective-permute-start.1) | collective-permute-done | bytes 262176 | tf_op jit(solution)/shard_map/ppermute | solution.py:424
  21.6 1.3 %collective-permute-start.9 = (bf16[256,512]{1,0:T(8,128)(2,1)S(1)}, bf16[256,512]{1,0:T(8,128)(2,1)S(1)}, u32[]{:S(2)}, u32[]{:S(2)}) collective-permute-start(bf16[256,512]{1,0:T(8,128)(2,1)S(1)} %collective-permute-done.8.refs_0_), channel_id=1, source_target_pairs={{0,1},{1,0},{2,3},{3,2},{4,5},{5,4},{6,7},{7,6},{8,9},{9,8},{10,11... | collective-permute-start | bytes 786440 | tf_op jit(solution)/shard_map/ppermute | solution.py:424
  22.9 0.0 collective-permute-done.11.refs_1_
  23.0 0.3 collective-permute-start.14
  23.3 0.0 collective-permute-done.6.refs_0_
  23.3 0.7 %collective-permute-start.7 = (bf16[256,512]{1,0:T(8,128)(2,1)S(1)}, bf16[256,512]{1,0:T(8,128)(2,1)S(1)}, u32[]{:S(2)}, u32[]{:S(2)}) collective-permute-start(bf16[256,512]{1,0:T(8,128)(2,1)S(1)} %collective-permute-done.6.refs_0_), channel_id=1, source_target_pairs={{0,1},{1,0},{2,3},{3,2},{4,5},{5,4},{6,7},{7,6},{8,9},{9,8},{10,11... | collective-permute-start | bytes 786440 | tf_op jit(solution)/shard_map/ppermute | solution.py:424
  24.0 0.0 collective-permute-done.10.refs_1_
  24.0 0.0 collective-permute-start.2
  24.0 0.2 collective-permute-done.3.refs_1_
  24.1 1.1 %collective-permute-start.4 = (bf16[256,512]{1,0:T(8,128)(2,1)S(1)}, bf16[256,512]{1,0:T(8,128)(2,1)S(1)}, u32[]{:S(2)}, u32[]{:S(2)}) collective-permute-start(bf16[256,512]{1,0:T(8,128)(2,1)S(1)} %collective-permute-done.3.refs_1_), channel_id=1, source_target_pairs={{0,1},{1,0},{2,3},{3,2},{4,5},{5,4},{6,7},{7,6},{8,9},{9,8},{10,11... | collective-permute-start | bytes 786440 | tf_op jit(solution)/shard_map/ppermute | solution.py:424
  25.2 0.0 collective-permute-done.9.refs_0_
  25.2 1.4 %collective-permute-start.13 = (bf16[96,512]{1,0:T(8,128)(2,1)S(1)}, bf16[96,512]{1,0:T(8,128)(2,1)S(1)}, u32[]{:S(2)}, u32[]{:S(2)}) collective-permute-start(bf16[96,512]{1,0:T(8,128)(2,1)S(1)} %slice.8), channel_id=1, source_target_pairs={{0,2},{1,3},{2,0},{3,1},{4,6},{5,7},{6,4},{7,5},{8,10},{9,11},{10,... | collective-permute-start | bytes 294920 | tf_op jit(solution)/shard_map/ppermute | solution.py:424
  26.7 2.1 %collective-permute-done.14.refs_1_.refs_3_ = bf16[160,512]{1,0:T(8,128)(2,1)S(1)} collective-permute-done((bf16[160,512]{1,0:T(8,128)(2,1)S(1)}, bf16[160,512]{1,0:T(8,128)(2,1)S(1)}, u32[]{:S(2)}, u32[]{:S(2)}) %collective-permute-start.14) | collective-permute-done | bytes 163872 | tf_op jit(solution)/shard_map/ppermute | solution.py:424
  28.8 0.9 %collective-permute-start.16 = (bf16[160,512]{1,0:T(8,128)(2,1)S(1)}, bf16[160,512]{1,0:T(8,128)(2,1)S(1)}, u32[]{:S(2)}, u32[]{:S(2)}) collective-permute-start(bf16[160,512]{1,0:T(8,128)(2,1)S(1)} %collective-permute-done.14.refs_1_.refs_3_), channel_id=1, source_target_pairs={{0,1},{1,0},{2,3},{3,2},{4,5},{5,4},{6,7},{7,6},{8,9},{9,8},{10,11... | collective-permute-start | bytes 491528 | tf_op jit(solution)/shard_map/ppermute | solution.py:424
  29.6 0.0 collective-permute-done.13.refs_0_.refs_2_
  29.6 0.9 %collective-permute-start.15 = (bf16[96,512]{1,0:T(8,128)(2,1)S(1)}, bf16[96,512]{1,0:T(8,128)(2,1)S(1)}, u32[]{:S(2)}, u32[]{:S(2)}) collective-permute-start(bf16[96,512]{1,0:T(8,128)(2,1)S(1)} %collective-permute-done.13.refs_0_.refs_2_), channel_id=1, source_target_pairs={{0,1},{1,0},{2,3},{3,2},{4,5},{5,4},{6,7},{7,6},{8,9},{9,8},{10,11... | collective-permute-start | bytes 294920 | tf_op jit(solution)/shard_map/ppermute | solution.py:424
  30.5 2.9 %prepare.1 = (f32[16,256]{1,0:T(8,128)S(1)}, f32[16,1024]{1,0:T(8,128)S(1)}, bf16[4,8,16,128]{3,2,1,0:T(8,128)(2,1)S(1)}, bf16[1024,1024]{1,0:T(8,128)(2,1)S(1)}, bf16[256,512]{1,0:T(8,128)(2,1)S(1)}) custom-call(s32[4,16]{1,0:T(4,128)} %bitcast.7, bf16[1024,1024]{1,0:T(8,128)(2,1)} %x_hbm.1, bf16[256,512]{1,0:T(8,128)(2,1)} %bitcast.6), custom_call_target="tpu_custom_call" | custom-call | tf_op jit(solution)/shard_map/prepare/pallas_call | solution.py:131
  33.4 1.4 %shard_map.37 = (f32[16,1280]{1,0:T(8,128)S(1)}, f32[16,128]{1,0:T(8,128)S(1)}, f32[256,1152]{1,0:T(8,128)S(1)}) custom-call(bf16[4,8,16,128]{3,2,1,0:T(8,128)(2,1)S(1)} %get-tuple-element.37.mask_ref, bf16[1024,1024]{1,0:T(8,128)(2,1)S(1)} %get-tuple-element.36.x_ref, bf16[256,512]{1,0:T(8,128)(2,1)S(1)} %get-tuple-element.38.refs_0_, ...), custom_call_target="tpu_custom_call" | custom-call | tf_op jit(solution)/shard_map/pallas_call | solution.py:270
  34.8 1.6 %shard_map.38 = (f32[16,1280]{1,0:T(8,128)S(1)}, f32[16,128]{1,0:T(8,128)S(1)}, f32[256,1152]{1,0:T(8,128)S(1)}) custom-call(bf16[4,8,16,128]{3,2,1,0:T(8,128)(2,1)S(1)} %get-tuple-element.37.mask_ref, bf16[1024,1024]{1,0:T(8,128)(2,1)S(1)} %get-tuple-element.36.x_ref, bf16[256,512]{1,0:T(8,128)(2,1)S(1)} %collective-permute-done.5.refs_0_, ...), custom_call_target="tpu_custom_call" | custom-call | tf_op jit(solution)/shard_map/pallas_call | solution.py:270
  36.5 1.5 %shard_map.39 = (f32[16,1280]{1,0:T(8,128)S(1)}, f32[16,128]{1,0:T(8,128)S(1)}, f32[256,1152]{1,0:T(8,128)S(1)}) custom-call(bf16[4,8,16,128]{3,2,1,0:T(8,128)(2,1)S(1)} %get-tuple-element.37.mask_ref, bf16[1024,1024]{1,0:T(8,128)(2,1)S(1)} %get-tuple-element.36.x_ref, bf16[256,512]{1,0:T(8,128)(2,1)S(1)} %collective-permute-done.8.refs_0_, ...), custom_call_target="tpu_custom_call" | custom-call | tf_op jit(solution)/shard_map/pallas_call | solution.py:270
  38.0 1.6 %shard_map.40 = (f32[16,1280]{1,0:T(8,128)S(1)}, f32[16,128]{1,0:T(8,128)S(1)}, f32[256,1152]{1,0:T(8,128)S(1)}) custom-call(bf16[4,8,16,128]{3,2,1,0:T(8,128)(2,1)S(1)} %get-tuple-element.37.mask_ref, bf16[1024,1024]{1,0:T(8,128)(2,1)S(1)} %get-tuple-element.36.x_ref, bf16[256,512]{1,0:T(8,128)(2,1)S(1)} %collective-permute-done.9.refs_0_, ...), custom_call_target="tpu_custom_call" | custom-call | tf_op jit(solution)/shard_map/pallas_call | solution.py:270
  39.5 0.8 %shard_map.41 = (f32[16,1280]{1,0:T(8,128)S(1)}, f32[16,128]{1,0:T(8,128)S(1)}, f32[256,1152]{1,0:T(8,128)S(1)}) custom-call(bf16[4,8,16,128]{3,2,1,0:T(8,128)(2,1)S(1)} %get-tuple-element.37.mask_ref, bf16[1024,1024]{1,0:T(8,128)(2,1)S(1)} %get-tuple-element.36.x_ref, bf16[256,512]{1,0:T(8,128)(2,1)S(1)} %collective-permute-done.6.refs_0_, ...), custom_call_target="tpu_custom_call" | custom-call | tf_op jit(solution)/shard_map/pallas_call | solution.py:270
  40.3 0.0 collective-permute-done.7.refs_2_
  40.3 2.1 %shard_map.42 = (f32[16,1280]{1,0:T(8,128)S(1)}, f32[16,128]{1,0:T(8,128)S(1)}, f32[256,1152]{1,0:T(8,128)S(1)}) custom-call(bf16[4,8,16,128]{3,2,1,0:T(8,128)(2,1)S(1)} %get-tuple-element.37.mask_ref, bf16[1024,1024]{1,0:T(8,128)(2,1)S(1)} %get-tuple-element.36.x_ref, bf16[256,512]{1,0:T(8,128)(2,1)S(1)} %collective-permute-done.1.refs_0_, ...), custom_call_target="tpu_custom_call" | custom-call | tf_op jit(solution)/shard_map/pallas_call | solution.py:270
  42.5 0.0 collective-permute-done.2.refs_0_
  42.5 0.0 collective-permute-done.4.refs_1_
  42.5 1.5 %shard_map.43 = (f32[16,1280]{1,0:T(8,128)S(1)}, f32[16,128]{1,0:T(8,128)S(1)}, f32[256,1152]{1,0:T(8,128)S(1)}) custom-call(bf16[4,8,16,128]{3,2,1,0:T(8,128)(2,1)S(1)} %get-tuple-element.37.mask_ref, bf16[1024,1024]{1,0:T(8,128)(2,1)S(1)} %get-tuple-element.36.x_ref, bf16[256,512]{1,0:T(8,128)(2,1)S(1)} %collective-permute-done.2.refs_0_, ...), custom_call_target="tpu_custom_call" | custom-call | tf_op jit(solution)/shard_map/pallas_call | solution.py:270
  44.0 0.0 collective-permute-done.15.refs_2_.refs_4_
  44.0 0.0 collective-permute-done.16.refs_3_.refs_5_
  44.0 1.0 %edge.1 = (f32[32,256]{1,0:T(8,128)S(1)}, bf16[256,1024]{1,0:T(8,128)(2,1)S(1)}, bf16[256,1024]{1,0:T(8,128)(2,1)S(1)}) custom-call(bf16[4,8,16,128]{3,2,1,0:T(8,128)(2,1)S(1)} %get-tuple-element.37.mask_ref, bf16[1024,1024]{1,0:T(8,128)(2,1)S(1)} %get-tuple-element.36.x_ref, f32[16,1280]{1,0:T(8,128)S(1)} %get-tuple-element.57.old_sum, ...), custom_call_target="tpu_custom_call" | custom-call | tf_op jit(solution)/shard_map/edge/pallas_call | solution.py:323
  45.0 1.9 %collective-permute-start.17 = (f32[32,256]{1,0:T(8,128)S(1)}, f32[32,256]{1,0:T(8,128)S(1)}, u32[]{:S(2)}, u32[]{:S(2)}) collective-permute-start(f32[32,256]{1,0:T(8,128)S(1)} %get-tuple-element.66), channel_id=1, source_target_pairs={{1,0},{2,1},{3,2},{4,3},{5,4},{6,5},{7,6},{8,7},{9,8},{10,9},{11,1... | collective-permute-start | bytes 98312 | tf_op jit(solution)/shard_map/ppermute | solution.py:424
  47.0 2.0 %last.1 = (f32[16,1024]{1,0:T(8,128)S(1)}, f32[16,128]{1,0:T(8,128)S(1)}) custom-call(bf16[1024,1024]{1,0:T(8,128)(2,1)S(1)} %get-tuple-element.36.x_ref, f32[16,1280]{1,0:T(8,128)S(1)} %get-tuple-element.57.old_sum, f32[16,128]{1,0:T(8,128)S(1)} %get-tuple-element.58.old_norm, f32[256,1152]{1,0:T(8,128)S(1)} %get-tuple-element.59.p_ref, ...), custom_call_target="tpu_custom_call" | custom-call | tf_op jit(solution)/shard_map/last/pallas_call | solution.py:374
  48.9 3.5 %collective-permute-done.17.after_ref = f32[32,256]{1,0:T(8,128)S(1)} collective-permute-done((f32[32,256]{1,0:T(8,128)S(1)}, f32[32,256]{1,0:T(8,128)S(1)}, u32[]{:S(2)}, u32[]{:S(2)}) %collective-permute-start.17) | collective-permute-done | bytes 32800 | tf_op jit(solution)/shard_map/ppermute | solution.py:424
  52.4 0.7 %finish.1 = f32[16,1024]{1,0:T(8,128)} custom-call(f32[16,1024]{1,0:T(8,128)S(1)} %get-tuple-element.63.main_ref, f32[16,128]{1,0:T(8,128)S(1)} %get-tuple-element.64.norm_ref, f32[16,1024]{1,0:T(8,128)S(1)} %get-tuple-element.65.energy_ref, f32[32,256]{1,0:T(8,128)S(1)} %collective-permute-done.17.after_ref), custom_call_target="tpu_custom_call" | custom-call | tf_op jit(solution)/shard_map/finish/pallas_call | solution.py:397
  (2 shorter events, 0.0 us)
Async XLA Ops:
  0.0 14.2 %collective-permute-start = (bf16[256,512]{1,0:T(8,128)(2,1)}, bf16[256,512]{1,0:T(8,128)(2,1)S(1)}, u32[]{:S(2)}, u32[]{:S(2)}) collective-permute-start(bf16[256,512]{1,0:T(8,128)(2,1)} %bitcast.2), channel_id=1, source_target_pairs={{0,8},{1,9},{2,10},{3,11},{4,12},{5,13},{6,14},{7,15},{8,0},{9,1},... | collective-permute-start | bytes 786440 | tf_op jit(solution)/shard_map/ppermute | solution.py:424
  2.3 12.2 %collective-permute-start.5 = (bf16[256,512]{1,0:T(8,128)(2,1)}, bf16[256,512]{1,0:T(8,128)(2,1)S(1)}, u32[]{:S(2)}, u32[]{:S(2)}) collective-permute-start(bf16[256,512]{1,0:T(8,128)(2,1)} %bitcast.3), channel_id=1, source_target_pairs={{0,2},{1,3},{2,0},{3,1},{4,6},{5,7},{6,4},{7,5},{8,10},{9,11},{10,... | collective-permute-start | bytes 786440 | tf_op jit(solution)/shard_map/ppermute | solution.py:424
  2.6 13.6 %collective-permute-start.12 = (bf16[256,512]{1,0:T(8,128)(2,1)}, bf16[256,512]{1,0:T(8,128)(2,1)S(1)}, u32[]{:S(2)}, u32[]{:S(2)}) collective-permute-start(bf16[256,512]{1,0:T(8,128)(2,1)} %bitcast.4), channel_id=1, source_target_pairs={{0,1},{1,0},{2,3},{3,2},{4,5},{5,4},{6,7},{7,6},{8,9},{9,8},{10,11... | collective-permute-start | bytes 786440 | tf_op jit(solution)/shard_map/ppermute | solution.py:424
  3.8 12.7 %collective-permute-start.8 = (bf16[256,512]{1,0:T(8,128)(2,1)}, bf16[256,512]{1,0:T(8,128)(2,1)S(1)}, u32[]{:S(2)}, u32[]{:S(2)}) collective-permute-start(bf16[256,512]{1,0:T(8,128)(2,1)} %bitcast.5), channel_id=1, source_target_pairs={{0,4},{1,5},{2,6},{3,7},{4,0},{5,1},{6,2},{7,3},{8,12},{9,13},{10,... | collective-permute-start | bytes 786440 | tf_op jit(solution)/shard_map/ppermute | solution.py:424
  14.2 7.4 %collective-permute-start.1 = (bf16[256,512]{1,0:T(8,128)(2,1)S(1)}, bf16[256,512]{1,0:T(8,128)(2,1)S(1)}, u32[]{:S(2)}, u32[]{:S(2)}) collective-permute-start(bf16[256,512]{1,0:T(8,128)(2,1)S(1)} %collective-permute-done.refs_1_), channel_id=1, source_target_pairs={{0,2},{1,3},{2,0},{3,1},{4,6},{5,7},{6,4},{7,5},{8,10},{9,11},{10,... | collective-permute-start | bytes 786440 | tf_op jit(solution)/shard_map/ppermute | solution.py:424
  14.5 8.5 %collective-permute-start.11 = (bf16[256,512]{1,0:T(8,128)(2,1)S(1)}, bf16[256,512]{1,0:T(8,128)(2,1)S(1)}, u32[]{:S(2)}, u32[]{:S(2)}) collective-permute-start(bf16[256,512]{1,0:T(8,128)(2,1)S(1)} %collective-permute-done.5.refs_0_), channel_id=1, source_target_pairs={{0,1},{1,0},{2,3},{3,2},{4,5},{5,4},{6,7},{7,6},{8,9},{9,8},{10,11... | collective-permute-start | bytes 786440 | tf_op jit(solution)/shard_map/ppermute | solution.py:424
  15.2 8.0 %collective-permute-start.6 = (bf16[256,512]{1,0:T(8,128)(2,1)S(1)}, bf16[256,512]{1,0:T(8,128)(2,1)S(1)}, u32[]{:S(2)}, u32[]{:S(2)}) collective-permute-start(bf16[256,512]{1,0:T(8,128)(2,1)S(1)} %collective-permute-done.5.refs_0_), channel_id=1, source_target_pairs={{0,4},{1,5},{2,6},{3,7},{4,0},{5,1},{6,2},{7,3},{8,12},{9,13},{10,... | collective-permute-start | bytes 786440 | tf_op jit(solution)/shard_map/ppermute | solution.py:424
  16.2 7.7 %collective-permute-start.10 = (bf16[256,512]{1,0:T(8,128)(2,1)S(1)}, bf16[256,512]{1,0:T(8,128)(2,1)S(1)}, u32[]{:S(2)}, u32[]{:S(2)}) collective-permute-start(bf16[256,512]{1,0:T(8,128)(2,1)S(1)} %collective-permute-done.refs_1_), channel_id=1, source_target_pairs={{0,1},{1,0},{2,3},{3,2},{4,5},{5,4},{6,7},{7,6},{8,9},{9,8},{10,11... | collective-permute-start | bytes 786440 | tf_op jit(solution)/shard_map/ppermute | solution.py:424
  16.5 7.6 %collective-permute-start.3 = (bf16[256,512]{1,0:T(8,128)(2,1)S(1)}, bf16[256,512]{1,0:T(8,128)(2,1)S(1)}, u32[]{:S(2)}, u32[]{:S(2)}) collective-permute-start(bf16[256,512]{1,0:T(8,128)(2,1)S(1)} %collective-permute-done.refs_1_), channel_id=1, source_target_pairs={{0,16},{1,17},{2,18},{3,19},{4,20},{5,21},{6,22},{7,23},{8,24},{9,... | collective-permute-start | bytes 786440 | tf_op jit(solution)/shard_map/ppermute | solution.py:424
  21.6 3.7 %collective-permute-start.9 = (bf16[256,512]{1,0:T(8,128)(2,1)S(1)}, bf16[256,512]{1,0:T(8,128)(2,1)S(1)}, u32[]{:S(2)}, u32[]{:S(2)}) collective-permute-start(bf16[256,512]{1,0:T(8,128)(2,1)S(1)} %collective-permute-done.8.refs_0_), channel_id=1, source_target_pairs={{0,1},{1,0},{2,3},{3,2},{4,5},{5,4},{6,7},{7,6},{8,9},{9,8},{10,11... | collective-permute-start | bytes 786440 | tf_op jit(solution)/shard_map/ppermute | solution.py:424
  23.0 5.8 %collective-permute-start.14 = (bf16[160,512]{1,0:T(8,128)(2,1)S(1)}, bf16[160,512]{1,0:T(8,128)(2,1)S(1)}, u32[]{:S(2)}, u32[]{:S(2)}) collective-permute-start(bf16[160,512]{1,0:T(8,128)(2,1)S(1)} %slice.9), channel_id=1, source_target_pairs={{0,16},{1,17},{2,18},{3,19},{4,20},{5,21},{6,22},{7,23},{8,24},{9,... | collective-permute-start | bytes 491528 | tf_op jit(solution)/shard_map/ppermute | solution.py:424
  23.3 17.1 %collective-permute-start.7 = (bf16[256,512]{1,0:T(8,128)(2,1)S(1)}, bf16[256,512]{1,0:T(8,128)(2,1)S(1)}, u32[]{:S(2)}, u32[]{:S(2)}) collective-permute-start(bf16[256,512]{1,0:T(8,128)(2,1)S(1)} %collective-permute-done.6.refs_0_), channel_id=1, source_target_pairs={{0,1},{1,0},{2,3},{3,2},{4,5},{5,4},{6,7},{7,6},{8,9},{9,8},{10,11... | collective-permute-start | bytes 786440 | tf_op jit(solution)/shard_map/ppermute | solution.py:424
  24.0 18.5 %collective-permute-start.2 = (bf16[256,512]{1,0:T(8,128)(2,1)S(1)}, bf16[256,512]{1,0:T(8,128)(2,1)S(1)}, u32[]{:S(2)}, u32[]{:S(2)}) collective-permute-start(bf16[256,512]{1,0:T(8,128)(2,1)S(1)} %collective-permute-done.1.refs_0_), channel_id=1, source_target_pairs={{0,1},{1,0},{2,3},{3,2},{4,5},{5,4},{6,7},{7,6},{8,9},{9,8},{10,11... | collective-permute-start | bytes 786440 | tf_op jit(solution)/shard_map/ppermute | solution.py:424
  24.1 18.3 %collective-permute-start.4 = (bf16[256,512]{1,0:T(8,128)(2,1)S(1)}, bf16[256,512]{1,0:T(8,128)(2,1)S(1)}, u32[]{:S(2)}, u32[]{:S(2)}) collective-permute-start(bf16[256,512]{1,0:T(8,128)(2,1)S(1)} %collective-permute-done.3.refs_1_), channel_id=1, source_target_pairs={{0,1},{1,0},{2,3},{3,2},{4,5},{5,4},{6,7},{7,6},{8,9},{9,8},{10,11... | collective-permute-start | bytes 786440 | tf_op jit(solution)/shard_map/ppermute | solution.py:424
  25.2 4.4 %collective-permute-start.13 = (bf16[96,512]{1,0:T(8,128)(2,1)S(1)}, bf16[96,512]{1,0:T(8,128)(2,1)S(1)}, u32[]{:S(2)}, u32[]{:S(2)}) collective-permute-start(bf16[96,512]{1,0:T(8,128)(2,1)S(1)} %slice.8), channel_id=1, source_target_pairs={{0,2},{1,3},{2,0},{3,1},{4,6},{5,7},{6,4},{7,5},{8,10},{9,11},{10,... | collective-permute-start | bytes 294920 | tf_op jit(solution)/shard_map/ppermute | solution.py:424
  28.8 15.2 %collective-permute-start.16 = (bf16[160,512]{1,0:T(8,128)(2,1)S(1)}, bf16[160,512]{1,0:T(8,128)(2,1)S(1)}, u32[]{:S(2)}, u32[]{:S(2)}) collective-permute-start(bf16[160,512]{1,0:T(8,128)(2,1)S(1)} %collective-permute-done.14.refs_1_.refs_3_), channel_id=1, source_target_pairs={{0,1},{1,0},{2,3},{3,2},{4,5},{5,4},{6,7},{7,6},{8,9},{9,8},{10,11... | collective-permute-start | bytes 491528 | tf_op jit(solution)/shard_map/ppermute | solution.py:424
  29.6 14.3 %collective-permute-start.15 = (bf16[96,512]{1,0:T(8,128)(2,1)S(1)}, bf16[96,512]{1,0:T(8,128)(2,1)S(1)}, u32[]{:S(2)}, u32[]{:S(2)}) collective-permute-start(bf16[96,512]{1,0:T(8,128)(2,1)S(1)} %collective-permute-done.13.refs_0_.refs_2_), channel_id=1, source_target_pairs={{0,1},{1,0},{2,3},{3,2},{4,5},{5,4},{6,7},{7,6},{8,9},{9,8},{10,11... | collective-permute-start | bytes 294920 | tf_op jit(solution)/shard_map/ppermute | solution.py:424
  45.0 7.4 %collective-permute-start.17 = (f32[32,256]{1,0:T(8,128)S(1)}, f32[32,256]{1,0:T(8,128)S(1)}, u32[]{:S(2)}, u32[]{:S(2)}) collective-permute-start(f32[32,256]{1,0:T(8,128)S(1)} %get-tuple-element.66), channel_id=1, source_target_pairs={{1,0},{2,1},{3,2},{4,3},{5,4},{6,5},{7,6},{8,7},{9,8},{10,9},{11,1... | collective-permute-start | bytes 98312 | tf_op jit(solution)/shard_map/ppermute | solution.py:424

commit v3 on v2

--- a/solution.py
+++ b/solution.py
@@ -382,25 +382,26 @@
     )(*[resident(value) for value in operands])
 
 
-def finish(main, norm, energy, after, scale_factor):
+def finish(main, norm, energy, after_core, after_chip, scale_factor):
     members, lags = main.shape
-    tap_count = after.shape[1]
+    tap_count = after_core.shape[1]
     tail = lags - tap_count
 
-    def kernel(main_ref, norm_ref, energy_ref, after_ref, out_ref):
+    def kernel(main_ref, norm_ref, energy_ref, core_ref, chip_ref, out_ref):
+        after = jnp.where(lax.axis_index("tm") % 2 == 0, core_ref[...], chip_ref[...])
         norms = jnp.sum(norm_ref[...], axis=1, keepdims=True)
         factor = lax.rsqrt(energy_ref[:, :tail] * norms + epsilon) * scale_factor
         out_ref[:, :tail] = main_ref[:, :tail] * factor
-        factor = lax.rsqrt((energy_ref[:, tail:] + after_ref[members:, :]) * norms + epsilon) * scale_factor
-        out_ref[:, tail:] = (main_ref[:, tail:] + after_ref[:members, :]) * factor
+        factor = lax.rsqrt((energy_ref[:, tail:] + after[members:, :]) * norms + epsilon) * scale_factor
+        out_ref[:, tail:] = (main_ref[:, tail:] + after[:members, :]) * factor
 
     return pl.pallas_call(
         kernel,
         out_shape=jax.ShapeDtypeStruct((members, lags), jnp.float32),
-        in_specs=[VMEM] * 4,
+        in_specs=[VMEM] * 5,
         compiler_params=PARAMS,
         name="finish",
-    )(resident(main), resident(norm), resident(energy), resident(after))
+    )(resident(main), resident(norm), resident(energy), resident(after_core), resident(after_chip))
 
 
 def per_device_chips(traces, templates, blocks):
@@ -436,7 +437,7 @@
         return send(value, lambda s, i: (s, i ^ 4))
 
     own = templates.reshape(local_taps * members, row_count)
-    part = own.shape[0] * 3 // 8
+    part = own.shape[0] * 5 // 8
     own_route, own_x_route, near_route, near_x_route = (0, 0), (2, 2), (4, 4), (6, 6)
     far_route, far_x_route, far_y_route, far_xy_route = (8, 12), (10, 14), (12, 8), (14, 10)
 
@@ -479,9 +480,10 @@
     pre, *wides = edge(
         masks, samples, ends, pair(far_xy_route), state[0], before, local_taps, tap_count
     )
-    after = send(pre, lambda s, i: (s, i - 1) if i > 0 else None)
+    after_core = over_core(pre)
+    after_chip = send(pre, lambda s, i: (s, i - 1) if i > 0 and i % 2 == 0 else None)
     main, norm = last(samples, wides, ends, pair(far_xy_route), state[0], local_taps, tap_count)
-    return finish(main, norm, energy, after, math.sqrt(tap_count * row_count))
+    return finish(main, norm, energy, after_core, after_chip, math.sqrt(tap_count * row_count))
 
 
 def fits(mesh, traces, templates, blocks):

time: 53.9 us -> 53.7 us (level)
  the two profiles are of different devices: /device:TPU:11 before, /device:TPU:23 now
where the time goes in v3:
time: 53.7 us; the launch traced here: 53.5 us
  waiting for transfers between devices  19.3 us (36%)
  Pallas kernels  17.1 us (32%)
  starting transfers between devices  16.9 us (31%)
    ppermute x19, waiting for transfers between devices, send(): return lax.ppermute(value, both, route)  19.3 us
    ppermute x19, starting transfers between devices, send(): return lax.ppermute(value, both, route)  16.9 us
    pallas_call x7, Pallas kernels, absorb(): pl.pallas_call(kernel, out_shape=shapes, in_specs=[VMEM] * len(operands),...  10.5 us
    pallas_call x1, Pallas kernels, prepare(): pl.pallas_call(kernel, out_shape=(pltpu.VMEM((members, tap_count), jnp.fl...  2.92 us
    pallas_call x1, Pallas kernels, last(): pl.pallas_call(kernel, out_shape=(pltpu.VMEM((members, lags), jnp.float32...  1.96 us
  transfers between devices with their start and end apart: 19, of which 7 were waited for; matrix products, arithmetic and copies ran while one was open for 0% of the time, Pallas kernels for 29%

profile of v3, /device:TPU:23, one launch (start us, length us, event | category | flops | bytes accessed | tf_op | source)
XLA Modules:
  0.0 53.5 jit_solution(9447948154454165759)
XLA Ops:
  0.0 0.2 collective-permute-start
  0.2 0.3 collective-permute-start.5
  0.4 1.2 %collective-permute-start.12 = (bf16[256,512]{1,0:T(8,128)(2,1)}, bf16[256,512]{1,0:T(8,128)(2,1)S(1)}, u32[]{:S(2)}, u32[]{:S(2)}) collective-permute-start(bf16[256,512]{1,0:T(8,128)(2,1)} %bitcast.4), channel_id=1, source_target_pairs={{0,1},{1,0},{2,3},{3,2},{4,5},{5,4},{6,7},{7,6},{8,9},{9,8},{10,11... | collective-permute-start | bytes 786440 | tf_op jit(solution)/shard_map/ppermute | solution.py:425
  1.7 1.1 %collective-permute-start.8 = (bf16[256,512]{1,0:T(8,128)(2,1)}, bf16[256,512]{1,0:T(8,128)(2,1)S(1)}, u32[]{:S(2)}, u32[]{:S(2)}) collective-permute-start(bf16[256,512]{1,0:T(8,128)(2,1)} %bitcast.5), channel_id=1, source_target_pairs={{0,4},{1,5},{2,6},{3,7},{4,0},{5,1},{6,2},{7,3},{8,12},{9,13},{10,... | collective-permute-start | bytes 786440 | tf_op jit(solution)/shard_map/ppermute | solution.py:425
  2.7 10.3 %collective-permute-done.refs_1_ = bf16[256,512]{1,0:T(8,128)(2,1)S(1)} collective-permute-done((bf16[256,512]{1,0:T(8,128)(2,1)}, bf16[256,512]{1,0:T(8,128)(2,1)S(1)}, u32[]{:S(2)}, u32[]{:S(2)}) %collective-permute-start) | collective-permute-done | bytes 262176 | tf_op jit(solution)/shard_map/ppermute | solution.py:425
  13.0 0.0 collective-permute-start.3
  13.0 0.0 collective-permute-done.5.refs_0_
  13.0 1.5 %collective-permute-start.11 = (bf16[256,512]{1,0:T(8,128)(2,1)S(1)}, bf16[256,512]{1,0:T(8,128)(2,1)S(1)}, u32[]{:S(2)}, u32[]{:S(2)}) collective-permute-start(bf16[256,512]{1,0:T(8,128)(2,1)S(1)} %collective-permute-done.5.refs_0_), channel_id=1, source_target_pairs={{0,1},{1,0},{2,3},{3,2},{4,5},{5,4},{6,7},{7,6},{8,9},{9,8},{10,11... | collective-permute-start | bytes 786440 | tf_op jit(solution)/shard_map/ppermute | solution.py:425
  14.6 2.7 %collective-permute-start.6 = (bf16[256,512]{1,0:T(8,128)(2,1)S(1)}, bf16[256,512]{1,0:T(8,128)(2,1)S(1)}, u32[]{:S(2)}, u32[]{:S(2)}) collective-permute-start(bf16[256,512]{1,0:T(8,128)(2,1)S(1)} %collective-permute-done.5.refs_0_), channel_id=1, source_target_pairs={{0,4},{1,5},{2,6},{3,7},{4,0},{5,1},{6,2},{7,3},{8,12},{9,13},{10,... | collective-permute-start | bytes 786440 | tf_op jit(solution)/shard_map/ppermute | solution.py:425
  17.2 0.0 collective-permute-done.12.refs_1_
  17.3 0.3 collective-permute-start.1
  17.5 0.0 collective-permute-done.8.refs_0_
  17.5 0.6 %collective-permute-start.10 = (bf16[256,512]{1,0:T(8,128)(2,1)S(1)}, bf16[256,512]{1,0:T(8,128)(2,1)S(1)}, u32[]{:S(2)}, u32[]{:S(2)}) collective-permute-start(bf16[256,512]{1,0:T(8,128)(2,1)S(1)} %collective-permute-done.refs_1_), channel_id=1, source_target_pairs={{0,1},{1,0},{2,3},{3,2},{4,5},{5,4},{6,7},{7,6},{8,9},{9,8},{10,11... | collective-permute-start | bytes 786440 | tf_op jit(solution)/shard_map/ppermute | solution.py:425
  18.1 1.3 %collective-permute-done.3.refs_1_ = bf16[256,512]{1,0:T(8,128)(2,1)S(1)} collective-permute-done((bf16[256,512]{1,0:T(8,128)(2,1)S(1)}, bf16[256,512]{1,0:T(8,128)(2,1)S(1)}, u32[]{:S(2)}, u32[]{:S(2)}) %collective-permute-start.3) | collective-permute-done | bytes 262176 | tf_op jit(solution)/shard_map/ppermute | solution.py:425
  19.4 2.4 %collective-permute-start.9 = (bf16[256,512]{1,0:T(8,128)(2,1)S(1)}, bf16[256,512]{1,0:T(8,128)(2,1)S(1)}, u32[]{:S(2)}, u32[]{:S(2)}) collective-permute-start(bf16[256,512]{1,0:T(8,128)(2,1)S(1)} %collective-permute-done.8.refs_0_), channel_id=1, source_target_pairs={{0,1},{1,0},{2,3},{3,2},{4,5},{5,4},{6,7},{7,6},{8,9},{9,8},{10,11... | collective-permute-start | bytes 786440 | tf_op jit(solution)/shard_map/ppermute | solution.py:425
  21.8 0.0 collective-permute-done.11.refs_1_
  21.8 0.3 collective-permute-start.13
  22.1 1.8 %collective-permute-done.6.refs_0_ = bf16[256,512]{1,0:T(8,128)(2,1)S(1)} collective-permute-done((bf16[256,512]{1,0:T(8,128)(2,1)S(1)}, bf16[256,512]{1,0:T(8,128)(2,1)S(1)}, u32[]{:S(2)}, u32[]{:S(2)}) %collective-permute-start.6) | collective-permute-done | bytes 262176 | tf_op jit(solution)/shard_map/ppermute | solution.py:425
  23.9 0.6 %collective-permute-start.7 = (bf16[256,512]{1,0:T(8,128)(2,1)S(1)}, bf16[256,512]{1,0:T(8,128)(2,1)S(1)}, u32[]{:S(2)}, u32[]{:S(2)}) collective-permute-start(bf16[256,512]{1,0:T(8,128)(2,1)S(1)} %collective-permute-done.6.refs_0_), channel_id=1, source_target_pairs={{0,1},{1,0},{2,3},{3,2},{4,5},{5,4},{6,7},{7,6},{8,9},{9,8},{10,11... | collective-permute-start | bytes 786440 | tf_op jit(solution)/shard_map/ppermute | solution.py:425
  24.5 0.3 collective-permute-done.1.refs_0_
  24.8 1.9 %collective-permute-start.2 = (bf16[256,512]{1,0:T(8,128)(2,1)S(1)}, bf16[256,512]{1,0:T(8,128)(2,1)S(1)}, u32[]{:S(2)}, u32[]{:S(2)}) collective-permute-start(bf16[256,512]{1,0:T(8,128)(2,1)S(1)} %collective-permute-done.1.refs_0_), channel_id=1, source_target_pairs={{0,1},{1,0},{2,3},{3,2},{4,5},{5,4},{6,7},{7,6},{8,9},{9,8},{10,11... | collective-permute-start | bytes 786440 | tf_op jit(solution)/shard_map/ppermute | solution.py:425
  26.7 0.0 collective-permute-done.10.refs_1_
  26.7 0.0 collective-permute-start.4
  26.7 0.0 collective-permute-done.9.refs_0_
  26.7 0.1 collective-permute-start.14
  26.8 1.5 %collective-permute-done.13.refs_0_.refs_2_ = bf16[160,512]{1,0:T(8,128)(2,1)S(1)} collective-permute-done((bf16[160,512]{1,0:T(8,128)(2,1)S(1)}, bf16[160,512]{1,0:T(8,128)(2,1)S(1)}, u32[]{:S(2)}, u32[]{:S(2)}) %collective-permute-start.13) | collective-permute-done | bytes 163872 | tf_op jit(solution)/shard_map/ppermute | solution.py:425
  28.3 1.1 %collective-permute-start.15 = (bf16[160,512]{1,0:T(8,128)(2,1)S(1)}, bf16[160,512]{1,0:T(8,128)(2,1)S(1)}, u32[]{:S(2)}, u32[]{:S(2)}) collective-permute-start(bf16[160,512]{1,0:T(8,128)(2,1)S(1)} %collective-permute-done.13.refs_0_.refs_2_), channel_id=1, source_target_pairs={{0,1},{1,0},{2,3},{3,2},{4,5},{5,4},{6,7},{7,6},{8,9},{9,8},{10,11... | collective-permute-start | bytes 491528 | tf_op jit(solution)/shard_map/ppermute | solution.py:425
  29.5 1.2 %collective-permute-done.14.refs_1_.refs_3_ = bf16[96,512]{1,0:T(8,128)(2,1)S(1)} collective-permute-done((bf16[96,512]{1,0:T(8,128)(2,1)S(1)}, bf16[96,512]{1,0:T(8,128)(2,1)S(1)}, u32[]{:S(2)}, u32[]{:S(2)}) %collective-permute-start.14) | collective-permute-done | bytes 98336 | tf_op jit(solution)/shard_map/ppermute | solution.py:425
  30.7 1.4 %collective-permute-start.16 = (bf16[96,512]{1,0:T(8,128)(2,1)S(1)}, bf16[96,512]{1,0:T(8,128)(2,1)S(1)}, u32[]{:S(2)}, u32[]{:S(2)}) collective-permute-start(bf16[96,512]{1,0:T(8,128)(2,1)S(1)} %collective-permute-done.14.refs_1_.refs_3_), channel_id=1, source_target_pairs={{0,1},{1,0},{2,3},{3,2},{4,5},{5,4},{6,7},{7,6},{8,9},{9,8},{10,11... | collective-permute-start | bytes 294920 | tf_op jit(solution)/shard_map/ppermute | solution.py:425
  32.0 2.9 %prepare.1 = (f32[16,256]{1,0:T(8,128)S(1)}, f32[16,1024]{1,0:T(8,128)S(1)}, bf16[4,8,16,128]{3,2,1,0:T(8,128)(2,1)S(1)}, bf16[1024,1024]{1,0:T(8,128)(2,1)S(1)}, bf16[256,512]{1,0:T(8,128)(2,1)S(1)}) custom-call(s32[4,16]{1,0:T(4,128)} %bitcast.7, bf16[1024,1024]{1,0:T(8,128)(2,1)} %x_hbm.1, bf16[256,512]{1,0:T(8,128)(2,1)} %bitcast.6), custom_call_target="tpu_custom_call" | custom-call | tf_op jit(solution)/shard_map/prepare/pallas_call | solution.py:131
  34.9 1.4 %shard_map.37 = (f32[16,1280]{1,0:T(8,128)S(1)}, f32[16,128]{1,0:T(8,128)S(1)}, f32[256,1152]{1,0:T(8,128)S(1)}) custom-call(bf16[4,8,16,128]{3,2,1,0:T(8,128)(2,1)S(1)} %get-tuple-element.37.mask_ref, bf16[1024,1024]{1,0:T(8,128)(2,1)S(1)} %get-tuple-element.36.x_ref, bf16[256,512]{1,0:T(8,128)(2,1)S(1)} %get-tuple-element.38.refs_0_, ...), custom_call_target="tpu_custom_call" | custom-call | tf_op jit(solution)/shard_map/pallas_call | solution.py:270
  36.4 1.6 %shard_map.38 = (f32[16,1280]{1,0:T(8,128)S(1)}, f32[16,128]{1,0:T(8,128)S(1)}, f32[256,1152]{1,0:T(8,128)S(1)}) custom-call(bf16[4,8,16,128]{3,2,1,0:T(8,128)(2,1)S(1)} %get-tuple-element.37.mask_ref, bf16[1024,1024]{1,0:T(8,128)(2,1)S(1)} %get-tuple-element.36.x_ref, bf16[256,512]{1,0:T(8,128)(2,1)S(1)} %collective-permute-done.5.refs_0_, ...), custom_call_target="tpu_custom_call" | custom-call | tf_op jit(solution)/shard_map/pallas_call | solution.py:270
  38.0 1.5 %shard_map.39 = (f32[16,1280]{1,0:T(8,128)S(1)}, f32[16,128]{1,0:T(8,128)S(1)}, f32[256,1152]{1,0:T(8,128)S(1)}) custom-call(bf16[4,8,16,128]{3,2,1,0:T(8,128)(2,1)S(1)} %get-tuple-element.37.mask_ref, bf16[1024,1024]{1,0:T(8,128)(2,1)S(1)} %get-tuple-element.36.x_ref, bf16[256,512]{1,0:T(8,128)(2,1)S(1)} %collective-permute-done.8.refs_0_, ...), custom_call_target="tpu_custom_call" | custom-call | tf_op jit(solution)/shard_map/pallas_call | solution.py:270
  39.5 1.6 %shard_map.40 = (f32[16,1280]{1,0:T(8,128)S(1)}, f32[16,128]{1,0:T(8,128)S(1)}, f32[256,1152]{1,0:T(8,128)S(1)}) custom-call(bf16[4,8,16,128]{3,2,1,0:T(8,128)(2,1)S(1)} %get-tuple-element.37.mask_ref, bf16[1024,1024]{1,0:T(8,128)(2,1)S(1)} %get-tuple-element.36.x_ref, bf16[256,512]{1,0:T(8,128)(2,1)S(1)} %collective-permute-done.9.refs_0_, ...), custom_call_target="tpu_custom_call" | custom-call | tf_op jit(solution)/shard_map/pallas_call | solution.py:270
  41.1 0.8 %shard_map.41 = (f32[16,1280]{1,0:T(8,128)S(1)}, f32[16,128]{1,0:T(8,128)S(1)}, f32[256,1152]{1,0:T(8,128)S(1)}) custom-call(bf16[4,8,16,128]{3,2,1,0:T(8,128)(2,1)S(1)} %get-tuple-element.37.mask_ref, bf16[1024,1024]{1,0:T(8,128)(2,1)S(1)} %get-tuple-element.36.x_ref, bf16[256,512]{1,0:T(8,128)(2,1)S(1)} %collective-permute-done.6.refs_0_, ...), custom_call_target="tpu_custom_call" | custom-call | tf_op jit(solution)/shard_map/pallas_call | solution.py:270
  41.8 0.0 collective-permute-done.7.refs_2_
  41.8 2.1 %shard_map.42 = (f32[16,1280]{1,0:T(8,128)S(1)}, f32[16,128]{1,0:T(8,128)S(1)}, f32[256,1152]{1,0:T(8,128)S(1)}) custom-call(bf16[4,8,16,128]{3,2,1,0:T(8,128)(2,1)S(1)} %get-tuple-element.37.mask_ref, bf16[1024,1024]{1,0:T(8,128)(2,1)S(1)} %get-tuple-element.36.x_ref, bf16[256,512]{1,0:T(8,128)(2,1)S(1)} %collective-permute-done.1.refs_0_, ...), custom_call_target="tpu_custom_call" | custom-call | tf_op jit(solution)/shard_map/pallas_call | solution.py:270
  44.0 0.0 collective-permute-done.2.refs_0_
  44.0 0.0 collective-permute-done.4.refs_1_
  44.0 1.5 %shard_map.43 = (f32[16,1280]{1,0:T(8,128)S(1)}, f32[16,128]{1,0:T(8,128)S(1)}, f32[256,1152]{1,0:T(8,128)S(1)}) custom-call(bf16[4,8,16,128]{3,2,1,0:T(8,128)(2,1)S(1)} %get-tuple-element.37.mask_ref, bf16[1024,1024]{1,0:T(8,128)(2,1)S(1)} %get-tuple-element.36.x_ref, bf16[256,512]{1,0:T(8,128)(2,1)S(1)} %collective-permute-done.2.refs_0_, ...), custom_call_target="tpu_custom_call" | custom-call | tf_op jit(solution)/shard_map/pallas_call | solution.py:270
  45.5 0.0 collective-permute-done.16.refs_3_.refs_5_
  45.5 0.0 collective-permute-done.15.refs_2_.refs_4_
  45.5 1.0 %edge.1 = (f32[32,256]{1,0:T(8,128)S(1)}, bf16[256,1024]{1,0:T(8,128)(2,1)S(1)}, bf16[256,1024]{1,0:T(8,128)(2,1)S(1)}) custom-call(bf16[4,8,16,128]{3,2,1,0:T(8,128)(2,1)S(1)} %get-tuple-element.37.mask_ref, bf16[1024,1024]{1,0:T(8,128)(2,1)S(1)} %get-tuple-element.36.x_ref, f32[16,1280]{1,0:T(8,128)S(1)} %get-tuple-element.57.old_sum, ...), custom_call_target="tpu_custom_call" | custom-call | tf_op jit(solution)/shard_map/edge/pallas_call | solution.py:323
  46.6 0.1 collective-permute-start.17
  46.6 1.3 %collective-permute-start.18 = (f32[32,256]{1,0:T(8,128)S(1)}, f32[32,256]{1,0:T(8,128)S(1)}, u32[]{:S(2)}, u32[]{:S(2)}) collective-permute-start(f32[32,256]{1,0:T(8,128)S(1)} %get-tuple-element.66), channel_id=1, source_target_pairs={{2,1},{4,3},{6,5},{8,7},{10,9},{12,11},{14,13},{18,17},{20,19},{22... | collective-permute-start | bytes 98312 | tf_op jit(solution)/shard_map/ppermute | solution.py:425
  47.9 2.0 %last.1 = (f32[16,1024]{1,0:T(8,128)S(1)}, f32[16,128]{1,0:T(8,128)S(1)}) custom-call(bf16[1024,1024]{1,0:T(8,128)(2,1)S(1)} %get-tuple-element.36.x_ref, f32[16,1280]{1,0:T(8,128)S(1)} %get-tuple-element.57.old_sum, f32[16,128]{1,0:T(8,128)S(1)} %get-tuple-element.58.old_norm, f32[256,1152]{1,0:T(8,128)S(1)} %get-tuple-element.59.p_ref, ...), custom_call_target="tpu_custom_call" | custom-call | tf_op jit(solution)/shard_map/last/pallas_call | solution.py:374
  49.9 0.0 collective-permute-done.17.core_ref
  49.9 2.9 %collective-permute-done.18.chip_ref = f32[32,256]{1,0:T(8,128)S(1)} collective-permute-done((f32[32,256]{1,0:T(8,128)S(1)}, f32[32,256]{1,0:T(8,128)S(1)}, u32[]{:S(2)}, u32[]{:S(2)}) %collective-permute-start.18) | collective-permute-done | bytes 32800 | tf_op jit(solution)/shard_map/ppermute | solution.py:425
  52.8 0.7 %finish.1 = f32[16,1024]{1,0:T(8,128)} custom-call(f32[16,1024]{1,0:T(8,128)S(1)} %get-tuple-element.63.main_ref, f32[16,128]{1,0:T(8,128)S(1)} %get-tuple-element.64.norm_ref, f32[16,1024]{1,0:T(8,128)S(1)} %get-tuple-element.65.energy_ref, f32[32,256]{1,0:T(8,128)S(1)} %collective-permute-done.17.core_ref, f32[32,256]{1,0:T(8,128)S(1)} %collective-permute-done.18.chip_ref), custom_call_target="tpu_custom_call" | custom-call | tf_op jit(solution)/shard_map/finish/pallas_call | solution.py:398
  (2 shorter events, 0.0 us)
Async XLA Ops:
  0.0 13.0 %collective-permute-start = (bf16[256,512]{1,0:T(8,128)(2,1)}, bf16[256,512]{1,0:T(8,128)(2,1)S(1)}, u32[]{:S(2)}, u32[]{:S(2)}) collective-permute-start(bf16[256,512]{1,0:T(8,128)(2,1)} %bitcast.2), channel_id=1, source_target_pairs={{0,8},{1,9},{2,10},{3,11},{4,12},{5,13},{6,14},{7,15},{8,0},{9,1},... | collective-permute-start | bytes 786440 | tf_op jit(solution)/shard_map/ppermute | solution.py:425
  0.2 12.9 %collective-permute-start.5 = (bf16[256,512]{1,0:T(8,128)(2,1)}, bf16[256,512]{1,0:T(8,128)(2,1)S(1)}, u32[]{:S(2)}, u32[]{:S(2)}) collective-permute-start(bf16[256,512]{1,0:T(8,128)(2,1)} %bitcast.3), channel_id=1, source_target_pairs={{0,2},{1,3},{2,0},{3,1},{4,6},{5,7},{6,4},{7,5},{8,10},{9,11},{10,... | collective-permute-start | bytes 786440 | tf_op jit(solution)/shard_map/ppermute | solution.py:425
  0.4 16.8 %collective-permute-start.12 = (bf16[256,512]{1,0:T(8,128)(2,1)}, bf16[256,512]{1,0:T(8,128)(2,1)S(1)}, u32[]{:S(2)}, u32[]{:S(2)}) collective-permute-start(bf16[256,512]{1,0:T(8,128)(2,1)} %bitcast.4), channel_id=1, source_target_pairs={{0,1},{1,0},{2,3},{3,2},{4,5},{5,4},{6,7},{7,6},{8,9},{9,8},{10,11... | collective-permute-start | bytes 786440 | tf_op jit(solution)/shard_map/ppermute | solution.py:425
  1.7 15.8 %collective-permute-start.8 = (bf16[256,512]{1,0:T(8,128)(2,1)}, bf16[256,512]{1,0:T(8,128)(2,1)S(1)}, u32[]{:S(2)}, u32[]{:S(2)}) collective-permute-start(bf16[256,512]{1,0:T(8,128)(2,1)} %bitcast.5), channel_id=1, source_target_pairs={{0,4},{1,5},{2,6},{3,7},{4,0},{5,1},{6,2},{7,3},{8,12},{9,13},{10,... | collective-permute-start | bytes 786440 | tf_op jit(solution)/shard_map/ppermute | solution.py:425
  13.0 6.3 %collective-permute-start.3 = (bf16[256,512]{1,0:T(8,128)(2,1)S(1)}, bf16[256,512]{1,0:T(8,128)(2,1)S(1)}, u32[]{:S(2)}, u32[]{:S(2)}) collective-permute-start(bf16[256,512]{1,0:T(8,128)(2,1)S(1)} %collective-permute-done.refs_1_), channel_id=1, source_target_pairs={{0,16},{1,17},{2,18},{3,19},{4,20},{5,21},{6,22},{7,23},{8,24},{9,... | collective-permute-start | bytes 786440 | tf_op jit(solution)/shard_map/ppermute | solution.py:425
  13.0 8.7 %collective-permute-start.11 = (bf16[256,512]{1,0:T(8,128)(2,1)S(1)}, bf16[256,512]{1,0:T(8,128)(2,1)S(1)}, u32[]{:S(2)}, u32[]{:S(2)}) collective-permute-start(bf16[256,512]{1,0:T(8,128)(2,1)S(1)} %collective-permute-done.5.refs_0_), channel_id=1, source_target_pairs={{0,1},{1,0},{2,3},{3,2},{4,5},{5,4},{6,7},{7,6},{8,9},{9,8},{10,11... | collective-permute-start | bytes 786440 | tf_op jit(solution)/shard_map/ppermute | solution.py:425
  14.6 9.4 %collective-permute-start.6 = (bf16[256,512]{1,0:T(8,128)(2,1)S(1)}, bf16[256,512]{1,0:T(8,128)(2,1)S(1)}, u32[]{:S(2)}, u32[]{:S(2)}) collective-permute-start(bf16[256,512]{1,0:T(8,128)(2,1)S(1)} %collective-permute-done.5.refs_0_), channel_id=1, source_target_pairs={{0,4},{1,5},{2,6},{3,7},{4,0},{5,1},{6,2},{7,3},{8,12},{9,13},{10,... | collective-permute-start | bytes 786440 | tf_op jit(solution)/shard_map/ppermute | solution.py:425
  17.3 7.6 %collective-permute-start.1 = (bf16[256,512]{1,0:T(8,128)(2,1)S(1)}, bf16[256,512]{1,0:T(8,128)(2,1)S(1)}, u32[]{:S(2)}, u32[]{:S(2)}) collective-permute-start(bf16[256,512]{1,0:T(8,128)(2,1)S(1)} %collective-permute-done.refs_1_), channel_id=1, source_target_pairs={{0,2},{1,3},{2,0},{3,1},{4,6},{5,7},{6,4},{7,5},{8,10},{9,11},{10,... | collective-permute-start | bytes 786440 | tf_op jit(solution)/shard_map/ppermute | solution.py:425
  17.5 9.2 %collective-permute-start.10 = (bf16[256,512]{1,0:T(8,128)(2,1)S(1)}, bf16[256,512]{1,0:T(8,128)(2,1)S(1)}, u32[]{:S(2)}, u32[]{:S(2)}) collective-permute-start(bf16[256,512]{1,0:T(8,128)(2,1)S(1)} %collective-permute-done.refs_1_), channel_id=1, source_target_pairs={{0,1},{1,0},{2,3},{3,2},{4,5},{5,4},{6,7},{7,6},{8,9},{9,8},{10,11... | collective-permute-start | bytes 786440 | tf_op jit(solution)/shard_map/ppermute | solution.py:425
  19.4 7.4 %collective-permute-start.9 = (bf16[256,512]{1,0:T(8,128)(2,1)S(1)}, bf16[256,512]{1,0:T(8,128)(2,1)S(1)}, u32[]{:S(2)}, u32[]{:S(2)}) collective-permute-start(bf16[256,512]{1,0:T(8,128)(2,1)S(1)} %collective-permute-done.8.refs_0_), channel_id=1, source_target_pairs={{0,1},{1,0},{2,3},{3,2},{4,5},{5,4},{6,7},{7,6},{8,9},{9,8},{10,11... | collective-permute-start | bytes 786440 | tf_op jit(solution)/shard_map/ppermute | solution.py:425
  21.8 6.6 %collective-permute-start.13 = (bf16[160,512]{1,0:T(8,128)(2,1)S(1)}, bf16[160,512]{1,0:T(8,128)(2,1)S(1)}, u32[]{:S(2)}, u32[]{:S(2)}) collective-permute-start(bf16[160,512]{1,0:T(8,128)(2,1)S(1)} %slice.8), channel_id=1, source_target_pairs={{0,2},{1,3},{2,0},{3,1},{4,6},{5,7},{6,4},{7,5},{8,10},{9,11},{10,... | collective-permute-start | bytes 491528 | tf_op jit(solution)/shard_map/ppermute | solution.py:425
  23.9 17.9 %collective-permute-start.7 = (bf16[256,512]{1,0:T(8,128)(2,1)S(1)}, bf16[256,512]{1,0:T(8,128)(2,1)S(1)}, u32[]{:S(2)}, u32[]{:S(2)}) collective-permute-start(bf16[256,512]{1,0:T(8,128)(2,1)S(1)} %collective-permute-done.6.refs_0_), channel_id=1, source_target_pairs={{0,1},{1,0},{2,3},{3,2},{4,5},{5,4},{6,7},{7,6},{8,9},{9,8},{10,11... | collective-permute-start | bytes 786440 | tf_op jit(solution)/shard_map/ppermute | solution.py:425
  24.8 19.1 %collective-permute-start.2 = (bf16[256,512]{1,0:T(8,128)(2,1)S(1)}, bf16[256,512]{1,0:T(8,128)(2,1)S(1)}, u32[]{:S(2)}, u32[]{:S(2)}) collective-permute-start(bf16[256,512]{1,0:T(8,128)(2,1)S(1)} %collective-permute-done.1.refs_0_), channel_id=1, source_target_pairs={{0,1},{1,0},{2,3},{3,2},{4,5},{5,4},{6,7},{7,6},{8,9},{9,8},{10,11... | collective-permute-start | bytes 786440 | tf_op jit(solution)/shard_map/ppermute | solution.py:425
  26.7 17.3 %collective-permute-start.4 = (bf16[256,512]{1,0:T(8,128)(2,1)S(1)}, bf16[256,512]{1,0:T(8,128)(2,1)S(1)}, u32[]{:S(2)}, u32[]{:S(2)}) collective-permute-start(bf16[256,512]{1,0:T(8,128)(2,1)S(1)} %collective-permute-done.3.refs_1_), channel_id=1, source_target_pairs={{0,1},{1,0},{2,3},{3,2},{4,5},{5,4},{6,7},{7,6},{8,9},{9,8},{10,11... | collective-permute-start | bytes 786440 | tf_op jit(solution)/shard_map/ppermute | solution.py:425
  26.7 3.9 %collective-permute-start.14 = (bf16[96,512]{1,0:T(8,128)(2,1)S(1)}, bf16[96,512]{1,0:T(8,128)(2,1)S(1)}, u32[]{:S(2)}, u32[]{:S(2)}) collective-permute-start(bf16[96,512]{1,0:T(8,128)(2,1)S(1)} %slice.9), channel_id=1, source_target_pairs={{0,16},{1,17},{2,18},{3,19},{4,20},{5,21},{6,22},{7,23},{8,24},{9,... | collective-permute-start | bytes 294920 | tf_op jit(solution)/shard_map/ppermute | solution.py:425
  28.3 17.2 %collective-permute-start.15 = (bf16[160,512]{1,0:T(8,128)(2,1)S(1)}, bf16[160,512]{1,0:T(8,128)(2,1)S(1)}, u32[]{:S(2)}, u32[]{:S(2)}) collective-permute-start(bf16[160,512]{1,0:T(8,128)(2,1)S(1)} %collective-permute-done.13.refs_0_.refs_2_), channel_id=1, source_target_pairs={{0,1},{1,0},{2,3},{3,2},{4,5},{5,4},{6,7},{7,6},{8,9},{9,8},{10,11... | collective-permute-start | bytes 491528 | tf_op jit(solution)/shard_map/ppermute | solution.py:425
  30.7 14.8 %collective-permute-start.16 = (bf16[96,512]{1,0:T(8,128)(2,1)S(1)}, bf16[96,512]{1,0:T(8,128)(2,1)S(1)}, u32[]{:S(2)}, u32[]{:S(2)}) collective-permute-start(bf16[96,512]{1,0:T(8,128)(2,1)S(1)} %collective-permute-done.14.refs_1_.refs_3_), channel_id=1, source_target_pairs={{0,1},{1,0},{2,3},{3,2},{4,5},{5,4},{6,7},{7,6},{8,9},{9,8},{10,11... | collective-permute-start | bytes 294920 | tf_op jit(solution)/shard_map/ppermute | solution.py:425
  46.6 3.3 %collective-permute-start.17 = (f32[32,256]{1,0:T(8,128)S(1)}, f32[32,256]{1,0:T(8,128)S(1)}, u32[]{:S(2)}, u32[]{:S(2)}) collective-permute-start(f32[32,256]{1,0:T(8,128)S(1)} %get-tuple-element.66), channel_id=1, source_target_pairs={{0,1},{1,0},{2,3},{3,2},{4,5},{5,4},{6,7},{7,6},{8,9},{9,8},{10,11... | collective-permute-start | bytes 98312 | tf_op jit(solution)/shard_map/ppermute | solution.py:425
  46.6 6.1 %collective-permute-start.18 = (f32[32,256]{1,0:T(8,128)S(1)}, f32[32,256]{1,0:T(8,128)S(1)}, u32[]{:S(2)}, u32[]{:S(2)}) collective-permute-start(f32[32,256]{1,0:T(8,128)S(1)} %get-tuple-element.66), channel_id=1, source_target_pairs={{2,1},{4,3},{6,5},{8,7},{10,9},{12,11},{14,13},{18,17},{20,19},{22... | collective-permute-start | bytes 98312 | tf_op jit(solution)/shard_map/ppermute | solution.py:425
